TPU v7x, 32 devices: a whole 2x2x4 slice. The times are simulated.
32 devices in a mesh: dp: 8 (over z, y), head: 4 (over x, core).
Axes of the slice: x: 2, y: 2, z: 4, core: 2. Of those that a mesh axis runs over, the one named last changes fastest.
Arguments:
- tokens: bfloat16 [8, 1024, 768], P('dp', 'head'), may hold values from -6 to 6
- memory: bfloat16 [8, 2048, 768], P('dp', 'head'), may hold values from -6 to 6
- text_length: int32 [8], P('dp'), may hold values from 256 to 1024, as said below
- patch_count: int32 [8], P('dp'), may hold values from 512 to 2048, as said below
- self_gain: bfloat16 [768], P(('dp', 'head')), may hold values from 0.5 to 1.5
- self_query: bfloat16 [768, 768], P(('dp', 'head')), may hold values from -0.21875 to 0.21875
- self_key: bfloat16 [768, 768], P(('dp', 'head')), may hold values from -0.21875 to 0.21875
- self_value: bfloat16 [768, 768], P(('dp', 'head')), may hold values from -0.21875 to 0.21875
- self_out: bfloat16 [768, 768], P(('dp', 'head')), may hold values from -3.5 to 3.5
- cross_gain: bfloat16 [768], P(('dp', 'head')), may hold values from 0.5 to 1.5
- cross_query: bfloat16 [768, 768], P(('dp', 'head')), may hold values from -0.21875 to 0.21875
- cross_key: bfloat16 [768, 768], P(('dp', 'head')), may hold values from -0.21875 to 0.21875
- cross_value: bfloat16 [768, 768], P(('dp', 'head')), may hold values from -0.21875 to 0.21875
- cross_out: bfloat16 [768, 768], P(('dp', 'head')), may hold values from -6 to 6
- mlp_gain: bfloat16 [768], P(('dp', 'head')), may hold values from 0.5 to 1.5
- mlp_gate: bfloat16 [768, 2048], P(('dp', 'head')), may hold values from -0.21875 to 0.21875
- mlp_up: bfloat16 [768, 2048], P(('dp', 'head')), may hold values from -0.21875 to 0.21875
- mlp_down: bfloat16 [2048, 768], P(('dp', 'head')), may hold values from -0.125 to 0.125
- output_grad: bfloat16 [8, 1024, 768], P('dp', 'head'), may hold values from -6 to 6
Outputs:
- output: bfloat16 [8, 1024, 768], P('dp', 'head')
- input_grad: float32 [8, 1024, 768], P('dp', 'head')
- memory_grad: float32 [8, 2048, 768], P('dp', 'head')
- self_dgain: float32 [768], P(('dp', 'head'))
- self_dquery: float32 [768, 768], P(('dp', 'head'))
- self_dkey: float32 [768, 768], P(('dp', 'head'))
- self_dvalue: float32 [768, 768], P(('dp', 'head'))
- self_dout: float32 [768, 768], P(('dp', 'head'))
- cross_dgain: float32 [768], P(('dp', 'head'))
- cross_dquery: float32 [768, 768], P(('dp', 'head'))
- cross_dkey: float32 [768, 768], P(('dp', 'head'))
- cross_dvalue: float32 [768, 768], P(('dp', 'head'))
- cross_dout: float32 [768, 768], P(('dp', 'head'))
- mlp_dgain: float32 [768], P(('dp', 'head'))
- mlp_dgate: float32 [768, 2048], P(('dp', 'head'))
- mlp_dup: float32 [768, 2048], P(('dp', 'head'))
- mlp_ddown: float32 [2048, 768], P(('dp', 'head'))
Inputs may be any that keep to these rules, and one draw needn't show every extreme that they name: `text_length`: positions at or past a chart's length are padding; some chart uses all 1024 positions and some only 256. `patch_count`: the valid patches are the first ones of a chart's grid; some chart fills all 2048 and some only 512.
All inputs are finite; a program needn't handle non-finite values.
Results may differ from a plain program's by a relative error of at most 0.02.
Values may be sent and summed in bfloat16 or wider, within the bound.
No kernel may reach another device: no remote copies, remote signals or barrier semaphores. Data moves between devices by JAX's collectives and lax.ppermute only.
A program may use at most 192 MiB of HBM per device.

v0:
```python
import math

import jax
import jax.numpy as jnp
from jax import lax
from jax.sharding import PartitionSpec as P

HEAD_DIM = 64


NEG_FILL = -1e30


def normalize(values, gain_vec):
    inverse = lax.rsqrt(jnp.mean(values * values, axis=-1, keepdims=True) + 1e-06)
    return values * inverse * gain_vec


def project(left_side, right_side):
    return jnp.einsum("gtd,de->gte", left_side, right_side, preferred_element_type=jnp.float32)


def back_project(left_side, right_side):
    return jnp.einsum("gte,de->gtd", left_side, right_side, preferred_element_type=jnp.float32)


def weight_term(left_side, right_side):
    return jnp.einsum("gtd,gte->de", left_side, right_side, preferred_element_type=jnp.float32)


def gated(gate_in, up_in):
    return jax.nn.gelu(gate_in, approximate=True) * up_in


def split_heads(values, groups):
    charts, row_count, feature_count = values.shape
    return values.reshape(charts, row_count, groups, feature_count // groups)


def heads_view(values, head_dim):
    charts, row_count, single, feature_count = values.shape
    return values.reshape(charts, row_count, single * feature_count // head_dim, head_dim)


def token_send(values):
    charts, row_count, heads_here, head_dim = values.shape
    return values.reshape(charts, row_count, 1, heads_here * head_dim)


def token_view(values):
    charts, row_count, groups, feature_count = values.shape
    return values.reshape(charts, row_count, groups * feature_count)


def key_mask(key_limit, first_row, block_rows, key_count, causal):
    columns = jnp.arange(key_count, dtype=jnp.int32)
    allowed = jnp.broadcast_to(columns[None, :] < key_limit, (block_rows, key_count))
    if causal:
        positions = first_row + jnp.arange(block_rows, dtype=jnp.int32)
        allowed = allowed & (columns[None, :] <= positions[:, None])
    return allowed


def chart_forward(query_rows, key_rows, value_rows, key_limit, causal):
    length, heads_here, head_dim = query_rows.shape
    block_rows = min(512, length)
    block_count = length // block_rows
    scaling = 1.0 / math.sqrt(head_dim)

    def one_block(block_pair):
        rows_block, first_row = block_pair
        scores = (
            jnp.einsum("qhd,khd->hqk", rows_block, key_rows, preferred_element_type=jnp.float32)
            * scaling
        )
        allowed = key_mask(key_limit, first_row, block_rows, key_rows.shape[0], causal)
        scores = jnp.where(allowed[None], scores, NEG_FILL)
        highest = jnp.max(scores, axis=-1, keepdims=True)
        exponent = jnp.exp(scores - highest)
        totals = jnp.sum(exponent, axis=-1, keepdims=True)
        prob_rows = (exponent / totals).astype(jnp.bfloat16)
        result = jnp.einsum(
            "hqk,khd->qhd", prob_rows, value_rows, preferred_element_type=jnp.float32
        )
        return (result.astype(jnp.bfloat16), (highest + jnp.log(totals))[..., 0])

    starts = jnp.arange(block_count, dtype=jnp.int32) * block_rows
    blocks_out, logsums = lax.map(
        one_block, (query_rows.reshape(block_count, block_rows, heads_here, head_dim), starts)
    )
    return (blocks_out.reshape(length, heads_here, head_dim), logsums)


def chart_backward(query_rows, key_rows, value_rows, key_limit, logsums, grad_rows, causal):
    length, heads_here, head_dim = query_rows.shape
    block_rows = min(512, length)
    block_count = length // block_rows
    scaling = 1.0 / math.sqrt(head_dim)

    def one_block(carried, block_pair):
        key_acc, value_acc = carried
        rows_block, log_block, grad_block, first_row = block_pair
        scores = (
            jnp.einsum("qhd,khd->hqk", rows_block, key_rows, preferred_element_type=jnp.float32)
            * scaling
        )
        allowed = key_mask(key_limit, first_row, block_rows, key_rows.shape[0], causal)
        scores = jnp.where(allowed[None], scores, NEG_FILL)
        prob_rows = jnp.exp(scores - log_block[..., None])
        prob_low = prob_rows.astype(jnp.bfloat16)
        grad_prob = jnp.einsum(
            "qhd,khd->hqk", grad_block, value_rows, preferred_element_type=jnp.float32
        )
        value_acc = value_acc + jnp.einsum(
            "hqk,qhd->khd", prob_low, grad_block, preferred_element_type=jnp.float32
        )
        centre = jnp.sum(prob_rows * grad_prob, axis=-1, keepdims=True)
        grad_score = (prob_rows * (grad_prob - centre)).astype(jnp.bfloat16)
        grad_query = (
            jnp.einsum("hqk,khd->qhd", grad_score, key_rows, preferred_element_type=jnp.float32)
            * scaling
        )
        key_acc = (
            key_acc
            + jnp.einsum("hqk,qhd->khd", grad_score, rows_block, preferred_element_type=jnp.float32)
            * scaling
        )
        return ((key_acc, value_acc), grad_query.astype(jnp.bfloat16))

    zero_rows = jnp.zeros(key_rows.shape, jnp.float32)
    starts = jnp.arange(block_count, dtype=jnp.int32) * block_rows
    shape_blocks = (block_count, block_rows, heads_here, head_dim)
    (key_acc, value_acc), grad_blocks = lax.scan(
        one_block,
        (zero_rows, zero_rows),
        (query_rows.reshape(shape_blocks), logsums, grad_rows.reshape(shape_blocks), starts),
    )
    return (
        grad_blocks.reshape(length, heads_here, head_dim),
        key_acc.astype(jnp.bfloat16),
        value_acc.astype(jnp.bfloat16),
    )


def on_device(
    tokens,
    memory,
    text_length,
    patch_count,
    self_gain,
    self_query,
    self_key,
    self_value,
    self_out,
    cross_gain,
    cross_query,
    cross_key,
    cross_value,
    cross_out,
    mlp_gain,
    mlp_gate,
    mlp_up,
    mlp_down,
    output_grad,
):
    groups = lax.axis_size("head")
    head_dim = HEAD_DIM
    gathered = (
        lax.all_gather(self_gain, ("dp", "head"), axis=0, tiled=True),
        lax.all_gather(self_query, ("dp", "head"), axis=0, tiled=True),
        lax.all_gather(self_key, ("dp", "head"), axis=0, tiled=True),
        lax.all_gather(self_value, ("dp", "head"), axis=0, tiled=True),
        lax.all_gather(self_out, ("dp", "head"), axis=0, tiled=True),
        lax.all_gather(cross_gain, ("dp", "head"), axis=0, tiled=True),
        lax.all_gather(cross_query, ("dp", "head"), axis=0, tiled=True),
        lax.all_gather(cross_key, ("dp", "head"), axis=0, tiled=True),
        lax.all_gather(cross_value, ("dp", "head"), axis=0, tiled=True),
        lax.all_gather(cross_out, ("dp", "head"), axis=0, tiled=True),
        lax.all_gather(mlp_gain, ("dp", "head"), axis=0, tiled=True),
        lax.all_gather(mlp_gate, ("dp", "head"), axis=0, tiled=True),
        lax.all_gather(mlp_up, ("dp", "head"), axis=0, tiled=True),
        lax.all_gather(mlp_down, ("dp", "head"), axis=0, tiled=True),
    )
    (
        gain_one,
        query_one,
        key_one,
        value_one,
        out_one,
        gain_two,
        query_two,
        key_two,
        value_two,
        out_two,
        gain_three,
        gate_three,
        up_three,
        down_three,
    ) = gathered
    text_float = tokens.astype(jnp.float32)
    scale_one = gain_one.astype(jnp.float32)
    normed_one = normalize(text_float, scale_one).astype(jnp.bfloat16)
    memory_keys = project(memory, key_two).astype(jnp.bfloat16)
    memory_values = project(memory, value_two).astype(jnp.bfloat16)
    memory_sent = (
        lax.all_to_all(
            split_heads(memory_keys, groups), "head", split_axis=2, concat_axis=1, tiled=True
        ),
        lax.all_to_all(
            split_heads(memory_values, groups), "head", split_axis=2, concat_axis=1, tiled=True
        ),
    )
    cross_keys = heads_view(memory_sent[0], head_dim)
    cross_values = heads_view(memory_sent[1], head_dim)
    token_queries = project(normed_one, query_one).astype(jnp.bfloat16)
    token_keys = project(normed_one, key_one).astype(jnp.bfloat16)
    token_values = project(normed_one, value_one).astype(jnp.bfloat16)
    self_sent = (
        lax.all_to_all(
            split_heads(token_queries, groups), "head", split_axis=2, concat_axis=1, tiled=True
        ),
        lax.all_to_all(
            split_heads(token_keys, groups), "head", split_axis=2, concat_axis=1, tiled=True
        ),
        lax.all_to_all(
            split_heads(token_values, groups), "head", split_axis=2, concat_axis=1, tiled=True
        ),
    )
    head_queries = heads_view(self_sent[0], head_dim)
    head_keys = heads_view(self_sent[1], head_dim)
    head_values = heads_view(self_sent[2], head_dim)
    self_context, self_logsums = lax.map(
        lambda pieces: chart_forward(pieces[0], pieces[1], pieces[2], pieces[3], True),
        (head_queries, head_keys, head_values, text_length),
    )
    context_one = token_view(
        lax.all_to_all(token_send(self_context), "head", split_axis=1, concat_axis=2, tiled=True)
    )
    hidden_one = text_float + project(context_one, out_one)
    scale_two = gain_two.astype(jnp.float32)
    normed_two = normalize(hidden_one, scale_two).astype(jnp.bfloat16)
    queries_two = project(normed_two, query_two).astype(jnp.bfloat16)
    cross_queries = heads_view(
        lax.all_to_all(
            split_heads(queries_two, groups), "head", split_axis=2, concat_axis=1, tiled=True
        ),
        head_dim,
    )
    cross_context, cross_logsums = lax.map(
        lambda pieces: chart_forward(pieces[0], pieces[1], pieces[2], pieces[3], False),
        (cross_queries, cross_keys, cross_values, patch_count),
    )
    context_two = token_view(
        lax.all_to_all(token_send(cross_context), "head", split_axis=1, concat_axis=2, tiled=True)
    )
    hidden_two = hidden_one + project(context_two, out_two)
    scale_three = gain_three.astype(jnp.float32)
    normed_three = normalize(hidden_two, scale_three).astype(jnp.bfloat16)
    gate_raw = project(normed_three, gate_three)
    up_raw = project(normed_three, up_three)
    mixed, mix_back = jax.vjp(gated, gate_raw, up_raw)
    mixed_low = mixed.astype(jnp.bfloat16)
    result_float = hidden_two + project(mixed_low, down_three)
    output = result_float.astype(jnp.bfloat16)
    back_weights = (
        lax.all_gather(self_gain, ("dp", "head"), axis=0, tiled=True),
        lax.all_gather(self_query, ("dp", "head"), axis=0, tiled=True),
        lax.all_gather(self_key, ("dp", "head"), axis=0, tiled=True),
        lax.all_gather(self_value, ("dp", "head"), axis=0, tiled=True),
        lax.all_gather(self_out, ("dp", "head"), axis=0, tiled=True),
        lax.all_gather(cross_gain, ("dp", "head"), axis=0, tiled=True),
        lax.all_gather(cross_query, ("dp", "head"), axis=0, tiled=True),
        lax.all_gather(cross_key, ("dp", "head"), axis=0, tiled=True),
        lax.all_gather(cross_value, ("dp", "head"), axis=0, tiled=True),
        lax.all_gather(cross_out, ("dp", "head"), axis=0, tiled=True),
        lax.all_gather(mlp_gain, ("dp", "head"), axis=0, tiled=True),
        lax.all_gather(mlp_gate, ("dp", "head"), axis=0, tiled=True),
        lax.all_gather(mlp_up, ("dp", "head"), axis=0, tiled=True),
        lax.all_gather(mlp_down, ("dp", "head"), axis=0, tiled=True),
    )
    (
        gain_one,
        query_one,
        key_one,
        value_one,
        out_one,
        gain_two,
        query_two,
        key_two,
        value_two,
        out_two,
        gain_three,
        gate_three,
        up_three,
        down_three,
    ) = back_weights
    grad_float = output_grad.astype(jnp.float32)
    grad_low = grad_float.astype(jnp.bfloat16)
    mlp_ddown = weight_term(mixed_low, grad_low)
    grad_mixed = back_project(grad_low, down_three)
    gate_back, up_back = mix_back(grad_mixed)
    gate_low = gate_back.astype(jnp.bfloat16)
    up_low = up_back.astype(jnp.bfloat16)
    mlp_dgate = weight_term(normed_three, gate_low)
    mlp_dup = weight_term(normed_three, up_low)
    grad_normed = back_project(gate_low, gate_three) + back_project(up_low, up_three)
    _, norm_back = jax.vjp(normalize, hidden_two, scale_three)
    part_two, mlp_dgain = norm_back(grad_normed)
    dhidden_two = grad_float + part_two
    branch_two = dhidden_two.astype(jnp.bfloat16)
    cross_dout = weight_term(context_two, branch_two)
    dcontext_two = back_project(branch_two, out_two).astype(jnp.bfloat16)
    cross_dheads = heads_view(
        lax.all_to_all(
            split_heads(dcontext_two, groups), "head", split_axis=2, concat_axis=1, tiled=True
        ),
        head_dim,
    )
    dquery_heads, dkey_heads, dvalue_heads = lax.map(
        lambda pieces: chart_backward(
            pieces[0], pieces[1], pieces[2], pieces[3], pieces[4], pieces[5], False
        ),
        (cross_queries, cross_keys, cross_values, patch_count, cross_logsums, cross_dheads),
    )
    returned = (
        lax.all_to_all(token_send(dquery_heads), "head", split_axis=1, concat_axis=2, tiled=True),
        lax.all_to_all(token_send(dkey_heads), "head", split_axis=1, concat_axis=2, tiled=True),
        lax.all_to_all(token_send(dvalue_heads), "head", split_axis=1, concat_axis=2, tiled=True),
    )
    dquery_tokens = token_view(returned[0])
    dkey_memory = token_view(returned[1])
    dvalue_memory = token_view(returned[2])
    cross_dquery = weight_term(normed_two, dquery_tokens)
    cross_dkey = weight_term(memory, dkey_memory)
    cross_dvalue = weight_term(memory, dvalue_memory)
    memory_grad = back_project(dkey_memory, key_two) + back_project(dvalue_memory, value_two)
    dnormed_two = back_project(dquery_tokens, query_two)
    _, norm_second = jax.vjp(normalize, hidden_one, scale_two)
    part_one, cross_dgain = norm_second(dnormed_two)
    dhidden_one = dhidden_two + part_one
    branch_one = dhidden_one.astype(jnp.bfloat16)
    self_dout = weight_term(context_one, branch_one)
    dcontext_one = back_project(branch_one, out_one).astype(jnp.bfloat16)
    self_dheads = heads_view(
        lax.all_to_all(
            split_heads(dcontext_one, groups), "head", split_axis=2, concat_axis=1, tiled=True
        ),
        head_dim,
    )
    dquery_heads, dkey_heads, dvalue_heads = lax.map(
        lambda pieces: chart_backward(
            pieces[0], pieces[1], pieces[2], pieces[3], pieces[4], pieces[5], True
        ),
        (head_queries, head_keys, head_values, text_length, self_logsums, self_dheads),
    )
    returned = (
        lax.all_to_all(token_send(dquery_heads), "head", split_axis=1, concat_axis=2, tiled=True),
        lax.all_to_all(token_send(dkey_heads), "head", split_axis=1, concat_axis=2, tiled=True),
        lax.all_to_all(token_send(dvalue_heads), "head", split_axis=1, concat_axis=2, tiled=True),
    )
    dquery_tokens = token_view(returned[0])
    dkey_tokens = token_view(returned[1])
    dvalue_tokens = token_view(returned[2])
    self_dquery = weight_term(normed_one, dquery_tokens)
    self_dkey = weight_term(normed_one, dkey_tokens)
    self_dvalue = weight_term(normed_one, dvalue_tokens)
    dnormed_one = (
        back_project(dquery_tokens, query_one)
        + back_project(dkey_tokens, key_one)
        + back_project(dvalue_tokens, value_one)
    )
    _, norm_first = jax.vjp(normalize, text_float, scale_one)
    part_zero, self_dgain = norm_first(dnormed_one)
    input_grad = dhidden_one + part_zero
    reduced = (
        lax.psum_scatter(self_dgain, ("dp", "head"), scatter_dimension=0, tiled=True),
        lax.psum_scatter(self_dquery, ("dp", "head"), scatter_dimension=0, tiled=True),
        lax.psum_scatter(self_dkey, ("dp", "head"), scatter_dimension=0, tiled=True),
        lax.psum_scatter(self_dvalue, ("dp", "head"), scatter_dimension=0, tiled=True),
        lax.psum_scatter(self_dout, ("dp", "head"), scatter_dimension=0, tiled=True),
        lax.psum_scatter(cross_dgain, ("dp", "head"), scatter_dimension=0, tiled=True),
        lax.psum_scatter(cross_dquery, ("dp", "head"), scatter_dimension=0, tiled=True),
        lax.psum_scatter(cross_dkey, ("dp", "head"), scatter_dimension=0, tiled=True),
        lax.psum_scatter(cross_dvalue, ("dp", "head"), scatter_dimension=0, tiled=True),
        lax.psum_scatter(cross_dout, ("dp", "head"), scatter_dimension=0, tiled=True),
        lax.psum_scatter(mlp_dgain, ("dp", "head"), scatter_dimension=0, tiled=True),
        lax.psum_scatter(mlp_dgate, ("dp", "head"), scatter_dimension=0, tiled=True),
        lax.psum_scatter(mlp_dup, ("dp", "head"), scatter_dimension=0, tiled=True),
        lax.psum_scatter(mlp_ddown, ("dp", "head"), scatter_dimension=0, tiled=True),
    )
    return (
        output,
        input_grad,
        memory_grad,
        reduced[0],
        reduced[1],
        reduced[2],
        reduced[3],
        reduced[4],
        reduced[5],
        reduced[6],
        reduced[7],
        reduced[8],
        reduced[9],
        reduced[10],
        reduced[11],
        reduced[12],
        reduced[13],
    )


def solution(mesh):
    in_specs = (
        P("dp", "head", None),
        P("dp", "head", None),
        P("dp"),
        P("dp"),
        P(("dp", "head")),
        P(("dp", "head"), None),
        P(("dp", "head"), None),
        P(("dp", "head"), None),
        P(("dp", "head"), None),
        P(("dp", "head")),
        P(("dp", "head"), None),
        P(("dp", "head"), None),
        P(("dp", "head"), None),
        P(("dp", "head"), None),
        P(("dp", "head")),
        P(("dp", "head"), None),
        P(("dp", "head"), None),
        P(("dp", "head"), None),
        P("dp", "head", None),
    )
    out_specs = (
        P("dp", "head", None),
        P("dp", "head", None),
        P("dp", "head", None),
        P(("dp", "head")),
        P(("dp", "head"), None),
        P(("dp", "head"), None),
        P(("dp", "head"), None),
        P(("dp", "head"), None),
        P(("dp", "head")),
        P(("dp", "head"), None),
        P(("dp", "head"), None),
        P(("dp", "head"), None),
        P(("dp", "head"), None),
        P(("dp", "head")),
        P(("dp", "head"), None),
        P(("dp", "head"), None),
        P(("dp", "head"), None),
    )
    return jax.shard_map(
        on_device, mesh=mesh, in_specs=in_specs, out_specs=out_specs, check_vma=False
    )
```

profile of v0, /device:TPU:0, one launch (start us, length us, event | category | flops | bytes accessed | tf_op | source)
XLA Modules:
  0.0 1868.5 jit_solution(11480789283955801562)
XLA Ops:
  15.9 42.1 %all-reduce.7 = (bf16[768]{0:T(1024)(128)(2,1)S(1)}, bf16[768]{0:T(1024)(128)(2,1)S(1)}, bf16[768]{0:T(1024)(128)(2,1)}) all-reduce(bf16[768]{0:T(1024)(128)(2,1)S(1)} %dynamic-update-slice, bf16[768]{0:T(1024)(128)(2,1)S(1)} %dynamic-update-slice.1, bf16[768]{0:T(1024)(128)(2,1)S(1)} %dynamic-update-slice.2), channel_id=1, replica_groups=mesh['dp'=8,'head'=4] {'dp','head'}, use_global_device_ids=true, to_apply=%add | all-reduce | flops 2304 | bytes 9216
  74.1 49.7 %all-gather.14.cloned.1.call-done = bf16[768,768]{1,0:T(8,128)(2,1)} async-done(((bf16[24,768]{1,0:T(8,128)(2,1)}), bf16[768,768]{1,0:T(8,128)(2,1)}) %all-gather.14.cloned.1.call-update) | async-done | bytes 1179664 | tf_op jit(solution)/shard_map/all_gather | solution.py:171
  130.0 49.7 %all-gather.16.cloned.1.call-done = bf16[768,768]{1,0:T(8,128)(2,1)} async-done(((bf16[24,768]{1,0:T(8,128)(2,1)}), bf16[768,768]{1,0:T(8,128)(2,1)}) %all-gather.16.cloned.1.call-update) | async-done | bytes 1179664 | tf_op jit(solution)/shard_map/all_gather | solution.py:172
  194.2 15.5 while.94
  242.2 49.1 %all-gather.24.cloned.1.call-done = bf16[768,768]{1,0:T(8,128)(2,1)} async-done(((bf16[24,768]{1,0:T(8,128)(2,1)}), bf16[768,768]{1,0:T(8,128)(2,1)}) %all-gather.24.cloned.1.call-update) | async-done | bytes 1179664 | tf_op jit(solution)/shard_map/all_gather | solution.py:177
  300.5 46.6 %all-gather.18.cloned.1.call-done = bf16[768,768]{1,0:T(8,128)(2,1)} async-done(((bf16[24,768]{1,0:T(8,128)(2,1)}), bf16[768,768]{1,0:T(8,128)(2,1)}) %all-gather.18.cloned.1.call-update) | async-done | bytes 1179664 | tf_op jit(solution)/shard_map/all_gather | solution.py:173
  349.1 53.9 %all-gather.20.cloned.1.call-done = bf16[768,768]{1,0:T(8,128)(2,1)} async-done(((bf16[24,768]{1,0:T(8,128)(2,1)}), bf16[768,768]{1,0:T(8,128)(2,1)}) %all-gather.20.cloned.1.call-update) | async-done | bytes 1179664 | tf_op jit(solution)/shard_map/all_gather | solution.py:175
  417.6 18.4 while.95
  473.5 46.3 %all-gather.28.cloned.1.call-done = bf16[768,2048]{1,0:T(8,128)(2,1)} async-done(((bf16[24,2048]{1,0:T(8,128)(2,1)}), bf16[768,2048]{1,0:T(8,128)(2,1)}) %all-gather.28.cloned.1.call-update) | async-done | bytes 3145744 | tf_op jit(solution)/shard_map/all_gather | solution.py:180
  524.2 56.1 %all-gather.30.cloned.1.call-done = bf16[768,2048]{1,0:T(8,128)(2,1)} async-done(((bf16[24,2048]{1,0:T(8,128)(2,1)}), bf16[768,2048]{1,0:T(8,128)(2,1)}) %all-gather.30.cloned.1.call-update) | async-done | bytes 3145744 | tf_op jit(solution)/shard_map/all_gather | solution.py:181
  584.6 56.3 %all-gather.32.cloned.1.call-done = bf16[2048,768]{1,0:T(8,128)(2,1)} async-done(((bf16[64,768]{1,0:T(8,128)(2,1)}), bf16[2048,768]{1,0:T(8,128)(2,1)}) %all-gather.32.cloned.1.call-update) | async-done | bytes 3145744 | tf_op jit(solution)/shard_map/all_gather | solution.py:182
  674.8 53.9 %while.96 = (s32[]{:T(128)}, f32[2048,3,64]{0,2,1:T(8,128)S(1)}, f32[2048,3,64]{0,2,1:T(8,128)}, bf16[2,512,3,64]{1,3,2,0:T(8,128)(2,1)}, bf16[2,512,3,64]{1,3,2...) while((s32[]{:T(128)}, f32[2048,3,64]{0,2,1:T(8,128)S(1)}, ...), condition=%wide.region_14.15_spmd.clone, body=%wide.region_12.14_spmd.clone.sunk | while | flops 2062615040 | bytes 190615984 | solution.py:133
  786.9 15.2 all_to_all.241
  875.7 38.1 %while.97 = (s32[]{:T(128)}, f32[1024,3,64]{0,2,1:T(8,128)S(1)}, f32[1024,3,64]{0,2,1:T(8,128)}, bf16[2,512,3,64]{1,3,2,0:T(8,128)(2,1)}, bf16[2,512,3,64]{1,3,2...) while((s32[]{:T(128)}, f32[1024,3,64]{0,2,1:T(8,128)S(1)}, ...), condition=%wide.region_18.19_spmd.clone, body=%wide.region_16.18_spmd.clone.sunk | while | flops 1032454144 | bytes 122276200 | solution.py:133
  921.2 13.2 all_to_all.242
  1009.3 39.2 %all-reduce.6 = (f32[768]{0:T(1024)S(1)}, f32[768]{0:T(1024)S(1)}, f32[768]{0:T(1024)S(1)}) all-reduce(f32[768]{0:T(1024)S(1)} %get-tuple-element.625, f32[768]{0:T(1024)S(1)} %get-tuple-element.623, f32[768]{0:T(1024)S(1)} %copy-done.69), channel_id=2, replica_groups=mesh['dp'=8,'head'=4] {'dp','head'}, use_global_device_ids=true, to_apply=%region_21.22.clone | all-reduce | flops 2304 | bytes 18432
  1051.4 32.1 %reduce-scatter.34.cloned.1.call-done = f32[24,768]{1,0:T(8,128)} async-done(((f32[768,768]{1,0:T(8,128)}), f32[24,768]{1,0:T(8,128)}) %reduce-scatter.34.cloned.1.call-update) | async-done | bytes 73744
  1083.5 103.8 %reduce-scatter.36.cloned.1.call-done = f32[24,768]{1,0:T(8,128)} async-done(((f32[768,768]{1,0:T(8,128)}), f32[24,768]{1,0:T(8,128)}) %reduce-scatter.36.cloned.1.call-update) | async-done | bytes 73744
  1187.3 104.7 %reduce-scatter.16.cloned.1.call-done = f32[24,768]{1,0:T(8,128)} async-done(((f32[768,768]{1,0:T(8,128)}), f32[24,768]{1,0:T(8,128)}) %reduce-scatter.16.cloned.1.call-update) | async-done | bytes 73744 | tf_op jit(solution)/shard_map/reduce_scatter | solution.py:377
  1292.0 103.8 %reduce-scatter.18.cloned.1.call-done = f32[24,768]{1,0:T(8,128)} async-done(((f32[768,768]{1,0:T(8,128)}), f32[24,768]{1,0:T(8,128)}) %reduce-scatter.18.cloned.1.call-update) | async-done | bytes 73744 | tf_op jit(solution)/shard_map/reduce_scatter | solution.py:378
  1395.8 104.8 %reduce-scatter.20.cloned.1.call-done = f32[24,768]{1,0:T(8,128)} async-done(((f32[768,768]{1,0:T(8,128)}), f32[24,768]{1,0:T(8,128)}) %reduce-scatter.20.cloned.1.call-update) | async-done | bytes 73744 | tf_op jit(solution)/shard_map/reduce_scatter | solution.py:379
  1500.6 119.7 %reduce-scatter.28.cloned.1.call-done = f32[24,2048]{1,0:T(8,128)} async-done(((f32[768,2048]{1,0:T(8,128)}), f32[24,2048]{1,0:T(8,128)}) %reduce-scatter.28.cloned.1.call-update) | async-done | bytes 196624 | tf_op jit(solution)/shard_map/reduce_scatter | solution.py:387
  1620.3 120.8 %reduce-scatter.30.cloned.1.call-done = f32[24,2048]{1,0:T(8,128)} async-done(((f32[768,2048]{1,0:T(8,128)}), f32[24,2048]{1,0:T(8,128)}) %reduce-scatter.30.cloned.1.call-update) | async-done | bytes 196624 | tf_op jit(solution)/shard_map/reduce_scatter | solution.py:388
  1741.1 120.0 %reduce-scatter.32.cloned.1.call-done = f32[64,768]{1,0:T(8,128)} async-done(((f32[2048,768]{1,0:T(8,128)}), f32[64,768]{1,0:T(8,128)}) %reduce-scatter.32.cloned.1.call-update) | async-done | bytes 196624 | tf_op jit(solution)/shard_map/reduce_scatter | solution.py:389
  (497 shorter events, 524.3 us)
Async XLA Ops:
  7.2 60.6 %all-gather.12.cloned.1.call-start = ((), (), s32[]{:S(2)}) async-start(), calls=%async_computation.27 | async-start | bytes 1216512 | tf_op jit(solution)/shard_map/all_gather | solution.py:170
  7.9 115.9 %all-gather.14.cloned.1.call-start = ((), (), s32[]{:S(2)}) async-start(), calls=%async_computation.28 | async-start | bytes 1216512 | tf_op jit(solution)/shard_map/all_gather | solution.py:171
  8.7 171.0 %all-gather.16.cloned.1.call-start = ((), (), s32[]{:S(2)}) async-start(), calls=%async_computation.29 | async-start | bytes 1216512 | tf_op jit(solution)/shard_map/all_gather | solution.py:172
  9.4 226.0 %all-gather.22.cloned.1.call-start = ((), (), s32[]{:S(2)}) async-start(), calls=%async_computation.32 | async-start | bytes 1216512 | tf_op jit(solution)/shard_map/all_gather | solution.py:176
  10.0 281.3 %all-gather.24.cloned.1.call-start = ((), (), s32[]{:S(2)}) async-start(), calls=%async_computation.33 | async-start | bytes 1216512 | tf_op jit(solution)/shard_map/all_gather | solution.py:177
  10.6 336.6 %all-gather.18.cloned.1.call-start = ((), (), s32[]{:S(2)}) async-start(), calls=%async_computation.30 | async-start | bytes 1216512 | tf_op jit(solution)/shard_map/all_gather | solution.py:173
  11.2 391.9 %all-gather.20.cloned.1.call-start = ((), (), s32[]{:S(2)}) async-start(), calls=%async_computation.31 | async-start | bytes 1216512 | tf_op jit(solution)/shard_map/all_gather | solution.py:175
  11.9 457.6 %all-gather.26.cloned.1.call-start = ((), (), s32[]{:S(2)}) async-start(), calls=%async_computation.34 | async-start | bytes 1216512 | tf_op jit(solution)/shard_map/all_gather | solution.py:178
  12.7 507.1 %all-gather.28.cloned.1.call-start = ((), (), s32[]{:S(2)}) async-start(), calls=%async_computation.35 | async-start | bytes 3244032 | tf_op jit(solution)/shard_map/all_gather | solution.py:180
  185.9 394.3 %all-gather.30.cloned.1.call-start = ((), (), s32[]{:S(2)}) async-start(), calls=%async_computation.36 | async-start | bytes 3244032 | tf_op jit(solution)/shard_map/all_gather | solution.py:181
  238.7 57.6 %all-to-all-start.5 = ((bf16[1,512,4,192]{1,3,0,2:T(8,128)(2,1)}), bf16[1,512,4,192]{1,3,0,2:T(8,128)(2,1)S(1)}, u32[]{:S(2)}, u32[]{:S(2)}) async-start(bf16[1,512,4,192]{1,3,0,2:T(8,128)(2,1)} %bitcast.34), calls=%async_computation.5 | async-start | bytes 1572864 | tf_op jit(solution)/shard_map/all_to_all | solution.py:206
  296.3 109.5 %all-to-all-start.6 = ((bf16[1,512,4,192]{1,3,0,2:T(8,128)(2,1)}), bf16[1,512,4,192]{1,3,0,2:T(8,128)(2,1)}, u32[]{:S(2)}, u32[]{:S(2)}) async-start(bf16[1,512,4,192]{1,3,0,2:T(8,128)(2,1)} %bitcast.485), calls=%async_computation.6 | async-start | bytes 1572864 | tf_op jit(solution)/shard_map/all_to_all | solution.py:209
  409.3 231.7 %all-gather.32.cloned.1.call-start = ((), (), s32[]{:S(2)}) async-start(), calls=%async_computation.37 | async-start | bytes 3244032 | tf_op jit(solution)/shard_map/all_gather | solution.py:182
  660.7 390.7 %reduce-scatter.26.cloned.1.call-start = ((), (), s32[]{:S(2)}) async-start(), calls=%async_computation.43 | async-start | bytes 2433024 | tf_op jit(solution)/shard_map/reduce_scatter | solution.py:385
  663.9 387.4 %reduce-scatter.22.cloned.1.call-start = ((), (), s32[]{:S(2)}) async-start(), calls=%async_computation.41 | async-start | bytes 2433024 | tf_op jit(solution)/shard_map/reduce_scatter | solution.py:380
  763.6 287.8 %reduce-scatter.24.cloned.1.call-start = ((), (), s32[]{:S(2)}) async-start(), calls=%async_computation.42 | async-start | bytes 2433024 | tf_op jit(solution)/shard_map/reduce_scatter | solution.py:382
  765.8 317.7 %reduce-scatter.34.cloned.1.call-start = ((), (), s32[]{:S(2)}) async-start(), calls=%async_computation.47 | async-start | bytes 2433024
  849.1 338.2 %reduce-scatter.36.cloned.1.call-start = ((), (), s32[]{:S(2)}) async-start(), calls=%async_computation.48 | async-start | bytes 2433024
  874.8 417.2 %reduce-scatter.16.cloned.1.call-start = ((), (), s32[]{:S(2)}) async-start(), calls=%async_computation.38 | async-start | bytes 2433024 | tf_op jit(solution)/shard_map/reduce_scatter | solution.py:377
  940.3 455.5 %reduce-scatter.18.cloned.1.call-start = ((), (), s32[]{:S(2)}) async-start(), calls=%async_computation.39 | async-start | bytes 2433024 | tf_op jit(solution)/shard_map/reduce_scatter | solution.py:378
  959.5 541.1 %reduce-scatter.20.cloned.1.call-start = ((), (), s32[]{:S(2)}) async-start(), calls=%async_computation.40 | async-start | bytes 2433024 | tf_op jit(solution)/shard_map/reduce_scatter | solution.py:379
  982.9 637.4 %reduce-scatter.28.cloned.1.call-start = ((), (), s32[]{:S(2)}) async-start(), calls=%async_computation.44 | async-start | bytes 6488064 | tf_op jit(solution)/shard_map/reduce_scatter | solution.py:387
  987.9 753.2 %reduce-scatter.30.cloned.1.call-start = ((), (), s32[]{:S(2)}) async-start(), calls=%async_computation.45 | async-start | bytes 6488064 | tf_op jit(solution)/shard_map/reduce_scatter | solution.py:388
  992.9 868.2 %reduce-scatter.32.cloned.1.call-start = ((), (), s32[]{:S(2)}) async-start(), calls=%async_computation.46 | async-start | bytes 6488064 | tf_op jit(solution)/shard_map/reduce_scatter | solution.py:389
  (104 other events, 1927.3 us)
Sparse Core Ops, SparseCore 0:
  10.9 56.8 all-gather.11
  70.7 53.0 all-gather.13
  126.7 52.9 all-gather.15
  182.5 52.9 all-gather.21
  238.2 53.0 all-gather.23
  294.1 53.0 all-gather.17
  350.1 52.9 all-gather.19
  406.0 53.0 all-gather.25
  461.9 57.8 all-gather.27
  522.5 57.7 all-gather.29
  583.1 57.7 all-gather.31
  667.1 99.1 reduce-scatter.25
  773.0 100.2 reduce-scatter.21
  879.0 99.9 reduce-scatter.23
  985.5 97.9 reduce-scatter.33
  1089.2 98.0 reduce-scatter.35
  1193.9 98.1 reduce-scatter.15
  1297.7 97.9 reduce-scatter.17
  1402.5 98.0 reduce-scatter.19
  1506.7 113.5 reduce-scatter.27
  1627.4 113.6 reduce-scatter.29
  1747.3 113.7 reduce-scatter.31
where the time goes:
time: 1880 us; the launch traced here: 1870 us
  waiting for transfers between devices  1270 us (68%)
  matrix products  160 us (9%)
  local copies, waits for them, and re-layouts  141 us (8%)
  blocking collectives  140 us (7%)
  other arithmetic  95.5 us (5%)
  starting transfers between devices  42.3 us (2%)
    unnamed x24, waiting for transfers between devices  143 us
    reduce_scatter x1, waiting for transfers between devices, on_device(): lax.psum_scatter(mlp_dup, ('dp', 'head'), scatter_dimension=0, tiled=True)  121 us
    reduce_scatter x1, waiting for transfers between devices, on_device(): lax.psum_scatter(mlp_ddown, ('dp', 'head'), scatter_dimension=0, tiled=True)  120 us
    reduce_scatter x1, waiting for transfers between devices, on_device(): lax.psum_scatter(mlp_dgate, ('dp', 'head'), scatter_dimension=0, tiled=True)  120 us
    reduce_scatter x1, waiting for transfers between devices, on_device(): lax.psum_scatter(self_dvalue, ('dp', 'head'), scatter_dimension=0, tiled=...  105 us
    reduce_scatter x1, waiting for transfers between devices, on_device(): lax.psum_scatter(self_dquery, ('dp', 'head'), scatter_dimension=0, tiled=...  105 us
    reduce_scatter x1, waiting for transfers between devices, on_device(): lax.psum_scatter(self_dkey, ('dp', 'head'), scatter_dimension=0, tiled=True)  104 us
    unnamed x2, blocking collectives  81.3 us
  transfers between devices with their start and end apart: 33, of which 23 were waited for; matrix products, arithmetic and copies ran while one was open for 19% of the time, Pallas kernels for 0%

commit v1 on v0

v1 whole, which is shorter than its diff:
```python
import functools
import math

import jax
import jax.numpy as jnp
from jax import lax
from jax.experimental import pallas as pl
from jax.experimental.pallas import tpu as pltpu
from jax.sharding import PartitionSpec as P

HEAD_DIM = 64
PAIR_LANES = 128
NEG_FILL = -1e30
EPS = 1e-06
F32 = jnp.float32
LOW = jnp.bfloat16


NT = (((1,), (1,)), ((), ()))
TN = (((0,), (0,)), ((), ()))


def dot_nt(left, right):
    return lax.dot_general(left, right, NT, preferred_element_type=F32)


def dot_tn(left, right):
    return lax.dot_general(left, right, TN, preferred_element_type=F32)


def dot_nn(left, right):
    return jnp.dot(left, right, preferred_element_type=F32)


def query_limits(info, queries, causal):
    last = info[0] - 1
    if not causal:
        return jnp.full((1, queries), last, jnp.int32), last
    rows = info[1] + lax.broadcasted_iota(jnp.int32, (1, queries), 1)
    return jnp.minimum(rows, last), jnp.minimum(info[1] + queries - 1, last)


def head_lanes(head):
    lanes = lax.broadcasted_iota(jnp.int32, (1, PAIR_LANES), 1)
    return (lanes // HEAD_DIM) == head


def fold(values, op):
    rows, columns = values.shape
    return op(values.reshape(rows // 8, 8, columns), axis=0)


def forward_kernel(causal, chunk, info, q_ref, k_ref, v_ref, c_ref, lse_ref, s_ref, m_ref, l_ref, a_ref):
    queries = q_ref.shape[0]
    chunks = k_ref.shape[0] // chunk
    scaling = 1.0 / math.sqrt(HEAD_DIM)
    limit, latest = query_limits(info, queries, causal)
    q_all = q_ref[...] * jnp.asarray(scaling, q_ref.dtype)
    q_heads = [jnp.where(head_lanes(h), q_all, jnp.zeros_like(q_all)) for h in range(2)]
    m_ref[...] = jnp.full(m_ref.shape, NEG_FILL, F32)
    l_ref[...] = jnp.zeros(l_ref.shape, F32)
    a_ref[...] = jnp.zeros(a_ref.shape, F32)

    @pl.loop(0, chunks)
    def _(j):
        start = info[2 + j]

        @pl.when(start <= latest)
        def _():
            rows = pl.ds(pl.multiple_of(j * chunk, chunk), chunk)
            keys = k_ref[rows, :]
            place = start + lax.broadcasted_iota(jnp.int32, (chunk, queries), 0)
            allowed = place <= limit
            for h in range(2):
                scores = jnp.where(allowed, dot_nt(keys, q_heads[h]), NEG_FILL)
                s_ref[h, rows, :] = scores
                m_ref[h] = jnp.maximum(m_ref[h], fold(scores, jnp.max))

    highest = [jnp.max(m_ref[h], axis=0, keepdims=True) for h in range(2)]

    @pl.loop(0, chunks)
    def _(j):
        @pl.when(info[2 + j] <= latest)
        def _():
            rows = pl.ds(pl.multiple_of(j * chunk, chunk), chunk)
            values = v_ref[rows, :]
            for h in range(2):
                weight = jnp.exp(s_ref[h, rows, :] - highest[h])
                l_ref[h] = l_ref[h] + fold(weight, jnp.sum)
                a_ref[h] = a_ref[h] + dot_tn(values, weight.astype(LOW))

    parts = []
    for h in range(2):
        total = jnp.sum(l_ref[h], axis=0, keepdims=True)
        lse_ref[0, pl.ds(h, 1), :] = highest[h] + jnp.log(total)
        parts.append(a_ref[h, pl.ds(h * HEAD_DIM, HEAD_DIM), :] / total)
    c_ref[...] = jnp.concatenate(parts, axis=0).T.astype(c_ref.dtype)


def backward_kernel(causal, chunk, info, q_ref, k_ref, v_ref, c_ref, g_ref, lse_ref, dq_ref, dk_ref, dv_ref, a_ref):
    queries = q_ref.shape[0]
    chunks = k_ref.shape[0] // chunk
    scaling = 1.0 / math.sqrt(HEAD_DIM)
    limit, latest = query_limits(info, queries, causal)
    q_all = q_ref[...] * jnp.asarray(scaling, q_ref.dtype)
    g_all = g_ref[...]
    q_heads = [jnp.where(head_lanes(h), q_all, jnp.zeros_like(q_all)) for h in range(2)]
    g_heads = [jnp.where(head_lanes(h), g_all, jnp.zeros_like(g_all)) for h in range(2)]
    product = (c_ref[...].astype(F32) * g_all.astype(F32)).T
    centres = [
        jnp.sum(product[h * HEAD_DIM : (h + 1) * HEAD_DIM], axis=0, keepdims=True) for h in range(2)
    ]
    logs = [lse_ref[0, pl.ds(h, 1), :] for h in range(2)]
    a_ref[...] = jnp.zeros(a_ref.shape, F32)

    @pl.loop(0, chunks)
    def _(j):
        start = info[2 + j]
        rows = pl.ds(pl.multiple_of(j * chunk, chunk), chunk)

        @pl.when(start <= latest)
        def _():
            keys = k_ref[rows, :]
            values = v_ref[rows, :]
            place = start + lax.broadcasted_iota(jnp.int32, (chunk, queries), 0)
            allowed = place <= limit
            dk = jnp.zeros((chunk, PAIR_LANES), F32)
            dv = jnp.zeros((chunk, PAIR_LANES), F32)
            for h in range(2):
                scores = jnp.where(allowed, dot_nt(keys, q_heads[h]), NEG_FILL)
                prob = jnp.exp(scores - logs[h])
                dprob = dot_nt(values, g_heads[h])
                dv = dv + dot_nn(prob.astype(LOW), g_heads[h])
                dscore = (prob * (dprob - centres[h])).astype(LOW)
                dk = dk + dot_nn(dscore, q_heads[h])
                a_ref[h] = a_ref[h] + dot_tn(keys, dscore)
            dk_ref[rows, :] = dk.astype(dk_ref.dtype)
            dv_ref[rows, :] = dv.astype(dv_ref.dtype)

        @pl.when(start > latest)
        def _():
            dk_ref[rows, :] = jnp.zeros((chunk, PAIR_LANES), dk_ref.dtype)
            dv_ref[rows, :] = jnp.zeros((chunk, PAIR_LANES), dv_ref.dtype)

    parts = [a_ref[h, pl.ds(h * HEAD_DIM, HEAD_DIM), :] for h in range(2)]
    dq_ref[...] = (jnp.concatenate(parts, axis=0).T * scaling).astype(dq_ref.dtype)


def lane_spec(rows):
    return pl.BlockSpec((rows, PAIR_LANES), lambda i, info: (0, i))


def stat_spec(queries):
    return pl.BlockSpec((1, 2, queries), lambda i, info: (i, 0, 0))


def attention_forward(info, queries, keys, values, causal, chunk):
    rows, features = queries.shape
    key_rows = keys.shape[0]
    pairs = features // PAIR_LANES
    return pl.pallas_call(
        functools.partial(forward_kernel, causal, chunk),
        out_shape=(
            jax.ShapeDtypeStruct((rows, features), LOW),
            jax.ShapeDtypeStruct((pairs, 2, rows), F32),
        ),
        grid_spec=pltpu.PrefetchScalarGridSpec(
            num_scalar_prefetch=1,
            grid=(pairs,),
            in_specs=[lane_spec(rows), lane_spec(key_rows), lane_spec(key_rows)],
            out_specs=[lane_spec(rows), stat_spec(rows)],
            scratch_shapes=[
                pltpu.VMEM((2, key_rows, rows), F32),
                pltpu.VMEM((2, 8, rows), F32),
                pltpu.VMEM((2, 8, rows), F32),
                pltpu.VMEM((2, PAIR_LANES, rows), F32),
            ],
        ),
        compiler_params=pltpu.CompilerParams(vmem_limit_bytes=40 << 20),
        cost_estimate=pl.CostEstimate(
            flops=16 * rows * key_rows * features,
            transcendentals=rows * key_rows * features // HEAD_DIM,
            bytes_accessed=4 * (rows + key_rows) * features,
        ),
    )(info, queries, keys, values)


def attention_backward(info, queries, keys, values, context, grads, lse, causal, chunk):
    rows, features = queries.shape
    key_rows = keys.shape[0]
    pairs = features // PAIR_LANES
    return pl.pallas_call(
        functools.partial(backward_kernel, causal, chunk),
        out_shape=(
            jax.ShapeDtypeStruct((rows, features), LOW),
            jax.ShapeDtypeStruct((key_rows, features), LOW),
            jax.ShapeDtypeStruct((key_rows, features), LOW),
        ),
        grid_spec=pltpu.PrefetchScalarGridSpec(
            num_scalar_prefetch=1,
            grid=(pairs,),
            in_specs=[
                lane_spec(rows),
                lane_spec(key_rows),
                lane_spec(key_rows),
                lane_spec(rows),
                lane_spec(rows),
                stat_spec(rows),
            ],
            out_specs=[lane_spec(rows), lane_spec(key_rows), lane_spec(key_rows)],
            scratch_shapes=[pltpu.VMEM((2, PAIR_LANES, rows), F32)],
        ),
        compiler_params=pltpu.CompilerParams(vmem_limit_bytes=40 << 20),
        cost_estimate=pl.CostEstimate(
            flops=40 * rows * key_rows * features,
            transcendentals=rows * key_rows * features // HEAD_DIM,
            bytes_accessed=8 * (rows + key_rows) * features,
        ),
    )(info, queries, keys, values, context, grads, lse)


def whole_kernel(count, rows, cuts, index, source, *targets):
    for step in range(count):
        at = index[step]
        for cut, target in zip(cuts, targets):
            target[pl.ds(step * rows, rows), :] = source[at, :, pl.ds(cut, target.shape[1])]


def halves_kernel(count, rows, cuts, index, *refs):
    sources, targets = refs[: len(cuts)], refs[len(cuts) :]
    half = count // 2
    for step in range(count):
        at = pl.ds(pl.multiple_of(index[step] * rows, rows), rows)
        for cut, source in zip(cuts, sources):
            targets[step // half][step % half, :, pl.ds(cut, source.shape[1])] = source[at, :]


def cuts_of(widths):
    return [sum(widths[:i]) for i in range(len(widths))]


def vmem_specs(number):
    return [pl.BlockSpec(memory_space=pltpu.VMEM)] * number


def to_whole(blocks, index, widths):
    count, rows, columns = blocks.shape
    cuts = cuts_of(widths)
    if rows % 16:
        whole = jnp.take(blocks, index, axis=0).reshape(count * rows, columns)
        return [whole[:, cut : cut + width] for cut, width in zip(cuts, widths)]
    return pl.pallas_call(
        functools.partial(whole_kernel, count, rows, cuts),
        out_shape=[jax.ShapeDtypeStruct((count * rows, width), blocks.dtype) for width in widths],
        in_specs=[pl.BlockSpec(memory_space=pltpu.SMEM)] + vmem_specs(1),
        out_specs=vmem_specs(len(widths)),
        cost_estimate=pl.CostEstimate(
            flops=0, transcendentals=0, bytes_accessed=4 * count * rows * columns
        ),
    )(index, blocks)


def to_halves(wholes, index, rows):
    widths = [whole.shape[1] for whole in wholes]
    columns = sum(widths)
    count = wholes[0].shape[0] // rows
    half = count // 2
    if rows % 16:
        joined = jnp.concatenate(wholes, axis=1).reshape(count, rows, columns)
        joined = jnp.take(joined, index, axis=0)
        return joined[:half], joined[half:]
    shape = jax.ShapeDtypeStruct((half, rows, columns), wholes[0].dtype)
    return pl.pallas_call(
        functools.partial(halves_kernel, count, rows, cuts_of(widths)),
        out_shape=[shape, shape],
        in_specs=[pl.BlockSpec(memory_space=pltpu.SMEM)] + vmem_specs(len(wholes)),
        out_specs=vmem_specs(2),
        cost_estimate=pl.CostEstimate(
            flops=0, transcendentals=0, bytes_accessed=4 * count * rows * columns
        ),
    )(index, *wholes)


def normalize(values):
    inverse = lax.rsqrt(jnp.mean(values * values, axis=-1, keepdims=True) + EPS)
    return values * inverse, inverse


def norm_back(normed, inverse, gain, grads):
    scaled = grads * gain
    return inverse * (scaled - normed * jnp.mean(scaled * normed, axis=-1, keepdims=True))


def gelu_parts(gate):
    factor = math.sqrt(2.0 / math.pi)
    inner = jnp.tanh(factor * (gate + 0.044715 * gate * gate * gate))
    value = 0.5 * gate * (1.0 + inner)
    slope = 0.5 * (1.0 + inner) + 0.5 * gate * (1.0 - inner * inner) * factor * (
        1.0 + 3.0 * 0.044715 * gate * gate
    )
    return value, slope


class Ring:
    def __init__(self):
        self.heads = lax.axis_size("head")
        self.charts = lax.axis_size("dp")
        self.groups = self.heads // 2
        place = lax.axis_index("head")
        self.second = (place % 2) == 1
        self.half = place % 2
        self.group = place // 2
        self.block = lax.axis_index("dp") * self.groups + self.group
        self.blocks = self.charts * self.groups
        chart_bits = [("dp", 1 << i) for i in range(self.charts.bit_length() - 1)]
        group_bits = [("head", 2 << i) for i in range(self.groups.bit_length() - 1)]
        far = chart_bits[1:]
        near = chart_bits[:1]
        self.group_bits = group_bits
        self.orders = (far + near + group_bits, far + group_bits + near)

    def send(self, values, axis, bit):
        size = self.charts if axis == "dp" else self.heads
        return lax.ppermute(values, axis, [(i, i ^ bit) for i in range(size)])

    def swap(self, values):
        return self.send(values, "head", 1)

    def in_order(self, mine, other):
        return jnp.where(self.second, other, mine), jnp.where(self.second, mine, other)

    def joined(self, mine, other, axis):
        return jnp.concatenate(self.in_order(mine, other), axis=axis)

    def masks(self, order):
        masks = [0]
        for axis, bit in order:
            step = bit * self.groups if axis == "dp" else bit // 2
            masks = masks + [m ^ step for m in masks]
        return masks

    def arrivals(self, order):
        apart = self.block ^ jnp.arange(self.blocks, dtype=jnp.int32)
        index = jnp.zeros((self.blocks,), jnp.int32)
        for place, (axis, bit) in enumerate(order):
            step = bit * self.groups if axis == "dp" else bit // 2
            index = index + jnp.where((apart & step) != 0, 1 << place, 0)
        return index

    def origins(self, order):
        return self.block ^ jnp.asarray(self.masks(order), jnp.int32)

    def gather(self, shard, order, widths):
        blocks = shard[None]
        for axis, bit in order:
            blocks = jnp.concatenate([blocks, self.send(blocks, axis, bit)], axis=0)
        return to_whole(blocks, self.arrivals(order), widths)

    def scatter_sum(self, wholes, order, rows):
        keep, give = to_halves(wholes, self.origins(order), rows)
        for place, (axis, bit) in enumerate(reversed(order)):
            got = self.send(give, axis, bit)
            half = keep.shape[0] // 2
            add = lambda cut: keep[cut].astype(F32) + got[cut].astype(F32)
            if half:
                give = add(slice(half, None)).astype(LOW)
                keep = add(slice(0, half)).astype(LOW)
            else:
                keep = add(slice(None))
        return keep[0]

    def pair_rows(self, mine, axis=0):
        return self.joined(mine, self.swap(mine), axis)

    def across(self, mine):
        rows = mine[None]
        for axis, bit in self.group_bits:
            rows = jnp.concatenate([rows, self.send(rows, axis, bit)], axis=0)
        return rows

    def halves(self, weights):
        first = jnp.concatenate([pair[0] for pair in weights], axis=1)
        later = jnp.concatenate([pair[1] for pair in weights], axis=1)
        mine = jnp.where(self.second, later, first)
        give = jnp.where(self.second, first, later)
        return self.joined(mine, self.swap(give), 0)

    def unhalve(self, pair_block):
        rows = pair_block.shape[0] // 2
        upper, lower = pair_block[:rows], pair_block[rows:]
        mine = jnp.where(self.second, lower, upper)
        give = jnp.where(self.second, upper, lower)
        return self.in_order(mine, self.swap(give))


def column_halves(weight):
    half = weight.shape[1] // 2
    return weight[:, :half], weight[:, half:]


def unit_halves(weight, units):
    rows, columns = weight.shape
    split = weight.reshape(rows, columns // (2 * units), 2, units)
    return split[:, :, 0].reshape(rows, -1), split[:, :, 1].reshape(rows, -1)


def unit_whole(first, later, units):
    rows, columns = first.shape
    pieces = [part.reshape(rows, columns // units, 1, units) for part in (first, later)]
    return jnp.concatenate(pieces, axis=2).reshape(rows, 2 * columns)


def on_device(
    tokens,
    memory,
    text_length,
    patch_count,
    self_gain,
    self_query,
    self_key,
    self_value,
    self_out,
    cross_gain,
    cross_query,
    cross_key,
    cross_value,
    cross_out,
    mlp_gain,
    mlp_gate,
    mlp_up,
    mlp_down,
    output_grad,
):
    ring = Ring()
    order_a, order_b = ring.orders
    width = tokens.shape[-1]
    half = width // 2
    units = mlp_down.shape[0]
    hidden_half = units * ring.blocks
    rows = self_query.shape[0]
    own = tokens.shape[1]
    own_patches = memory.shape[1]
    both = 2 * own

    gain_columns = jnp.stack([self_gain, cross_gain, mlp_gain], axis=1)
    gain_columns = jnp.pad(gain_columns, ((0, 0), (0, PAIR_LANES - 3)))
    first_a = ring.halves([column_halves(self_query), (gain_columns, gain_columns)])
    first_b = ring.halves([column_halves(self_key), column_halves(self_value)])
    token_rows = ring.pair_rows(ring.across(tokens[0]), 1).reshape(-1, width)
    query_one, gains = ring.gather(first_a, order_a, [half, PAIR_LANES])
    key_one, value_one = ring.gather(first_b, order_b, [half, half])
    patch_rows = ring.pair_rows(ring.across(memory[0]), 1).reshape(-1, width)
    next_a = ring.halves(
        [column_halves(self_out), column_halves(cross_query), column_halves(cross_out)]
    )
    next_b = ring.halves([column_halves(cross_key), column_halves(cross_value)])
    out_one_half, query_two, out_two_half = ring.gather(next_a, order_a, [half] * 3)
    key_two, value_two = ring.gather(next_b, order_b, [half] * 2)
    out_one = ring.pair_rows(out_one_half, 1)
    out_two = ring.pair_rows(out_two_half, 1)
    gate_rows = ring.halves([unit_halves(mlp_gate, units)])
    up_rows = ring.halves([unit_halves(mlp_up, units)])
    (gate_three,) = ring.gather(gate_rows, order_a, [hidden_half])
    (up_three,) = ring.gather(up_rows, order_b, [hidden_half])
    (down_left,) = ring.gather(mlp_down[:, :half], order_a, [half])
    (down_right,) = ring.gather(mlp_down[:, half:], order_b, [half])
    down_three = jnp.concatenate([down_left, down_right], axis=1)
    grad_low = ring.pair_rows(output_grad[0])

    gain_rows = gains[:, :3].astype(F32).T
    gain_one, gain_two, gain_three = gain_rows[0:1], gain_rows[1:2], gain_rows[2:3]

    token_chunk = math.gcd(256, both)
    patch_chunk = math.gcd(256, 2 * own_patches)

    def chunk_starts(rows_of_pair, chunk):
        groups = ring.group ^ jnp.arange(ring.groups, dtype=jnp.int32)
        inner = jnp.arange(rows_of_pair // chunk, dtype=jnp.int32) * chunk
        return (groups[:, None] * rows_of_pair + inner[None, :]).reshape(-1)

    first_query = (ring.group * both).astype(jnp.int32)[None]
    info_one = jnp.concatenate([text_length, first_query, chunk_starts(both, token_chunk)])
    info_two = jnp.concatenate(
        [patch_count, first_query, chunk_starts(2 * own_patches, patch_chunk)]
    )

    token_float = token_rows.astype(F32)
    plain_one, inverse_one = normalize(token_float)
    normed_one = (plain_one * gain_one).astype(LOW)
    mine_one = normed_one[:both]
    query_heads = dot_nn(mine_one, query_one).astype(LOW)
    key_heads = dot_nn(normed_one, key_one).astype(LOW)
    value_heads = dot_nn(normed_one, value_one).astype(LOW)
    context_heads, lse_one = attention_forward(
        info_one, query_heads, key_heads, value_heads, True, token_chunk
    )
    context_one = ring.pair_rows(context_heads, 1)
    hidden_one = token_float[:both] + dot_nn(context_one, out_one)
    plain_two, inverse_two = normalize(hidden_one)
    normed_two = (plain_two * gain_two).astype(LOW)
    cross_heads = dot_nn(normed_two, query_two).astype(LOW)
    memory_keys = dot_nn(patch_rows, key_two).astype(LOW)
    memory_values = dot_nn(patch_rows, value_two).astype(LOW)
    cross_context, lse_two = attention_forward(
        info_two, cross_heads, memory_keys, memory_values, False, patch_chunk
    )
    context_two = ring.pair_rows(cross_context, 1)
    hidden_two = hidden_one + dot_nn(context_two, out_two)
    plain_three, inverse_three = normalize(hidden_two)
    normed_three = (plain_three * gain_three).astype(LOW)
    gate = dot_nn(normed_three, gate_three)
    up = dot_nn(normed_three, up_three)
    active, slope = gelu_parts(gate)
    mixed = (active * up).astype(LOW)

    def own_rows(values, count):
        return lax.dynamic_slice_in_dim(values, ring.half * count, count, 0)

    def other_rows(values, count):
        return lax.dynamic_slice_in_dim(values, (1 - ring.half) * count, count, 0)

    down_part = dot_nn(mixed, down_three)
    down_got = ring.swap(other_rows(down_part, own).astype(LOW))
    output = (
        own_rows(hidden_two, own) + own_rows(down_part, own) + down_got.astype(F32)
    ).astype(LOW)

    grad_float = grad_low.astype(F32)
    ddown = dot_tn(mixed, grad_low).astype(LOW)
    grad_mixed = dot_nt(grad_low, down_three)
    gate_low = (grad_mixed * up * slope).astype(LOW)
    up_low = (grad_mixed * active).astype(LOW)
    dgate = dot_tn(normed_three, gate_low).astype(LOW)
    dup = dot_tn(normed_three, up_low).astype(LOW)
    part_three = dot_nt(gate_low, gate_three) + dot_nt(up_low, up_three)
    mlp_dgain = jnp.sum(part_three * plain_three, axis=0)
    part_low = part_three.astype(LOW)
    dnormed_three = part_low.astype(F32) + ring.swap(part_low).astype(F32)
    dhidden_two = grad_float + norm_back(plain_three, inverse_three, gain_three, dnormed_three)
    branch_two = dhidden_two.astype(LOW)
    mlp_dgate = ring.scatter_sum([dgate], order_a, 2 * rows)
    mlp_dup = ring.scatter_sum([dup], order_b, 2 * rows)
    ddown_left = ring.scatter_sum([ddown[:, :half]], order_a, units)
    ddown_right = ring.scatter_sum([ddown[:, half:]], order_b, units)
    mlp_ddown = jnp.concatenate([ddown_left, ddown_right], axis=1)

    def own_columns(values):
        return lax.dynamic_slice_in_dim(values, ring.half * half, half, 1)

    dcontext_two = dot_nt(branch_two, own_rows(out_two, half)).astype(LOW)
    dout_two = dot_tn(context_two, own_columns(branch_two)).astype(LOW)
    dquery, dkey, dvalue = attention_backward(
        info_two,
        cross_heads,
        memory_keys,
        memory_values,
        cross_context,
        dcontext_two,
        lse_two,
        False,
        patch_chunk,
    )
    part_two = dot_nt(dquery, query_two)
    cross_dgain = jnp.sum(part_two * plain_two, axis=0)
    part_low = part_two.astype(LOW)
    dnormed_two = part_low.astype(F32) + ring.swap(part_low).astype(F32)
    dhidden_one = dhidden_two + norm_back(plain_two, inverse_two, gain_two, dnormed_two)
    branch_one = dhidden_one.astype(LOW)
    dquery_two = dot_tn(normed_two, dquery).astype(LOW)
    dkey_two = dot_tn(patch_rows, dkey).astype(LOW)
    dvalue_two = dot_tn(patch_rows, dvalue).astype(LOW)
    cross_a = ring.scatter_sum([dout_two, dquery_two], order_a, 2 * rows)
    cross_b = ring.scatter_sum([dkey_two, dvalue_two], order_b, 2 * rows)

    def to_owner(part, count):
        part = part.reshape(ring.groups, 2, count, width)
        first, later = part[:, 0], part[:, 1]
        keep = jnp.where(ring.second, later, first)
        give = jnp.where(ring.second, first, later).astype(LOW)
        total = keep + ring.swap(give).astype(F32)
        for axis, bit in reversed(ring.group_bits):
            middle = total.shape[0] // 2
            total = total[:middle] + ring.send(total[middle:].astype(LOW), axis, bit).astype(F32)
        return total[0]

    memory_grad = to_owner(dot_nt(dkey, key_two) + dot_nt(dvalue, value_two), own_patches)

    dcontext_one = dot_nt(branch_one, own_rows(out_one, half)).astype(LOW)
    dout_one = dot_tn(context_one, own_columns(branch_one)).astype(LOW)
    dquery, dkey, dvalue = attention_backward(
        info_one,
        query_heads,
        key_heads,
        value_heads,
        context_heads,
        dcontext_one,
        lse_one,
        True,
        token_chunk,
    )
    dquery_one = dot_tn(mine_one, dquery).astype(LOW)
    dkey_one = dot_tn(normed_one, dkey).astype(LOW)
    dvalue_one = dot_tn(normed_one, dvalue).astype(LOW)
    part_one = dot_nt(dkey, key_one) + dot_nt(dvalue, value_one)
    part_mine = part_one[:both] + dot_nt(dquery, query_one)
    part_one = jnp.concatenate([part_mine, part_one[both:]], axis=0)
    self_dgain = jnp.sum(part_one * plain_one, axis=0)
    dgains = jnp.stack([self_dgain, cross_dgain, mlp_dgain], axis=1)
    dgains = jnp.pad(dgains, ((0, 0), (0, PAIR_LANES - 3))).astype(LOW)
    self_a = ring.scatter_sum([dquery_one, dout_one, dgains], order_a, 2 * rows)
    self_b = ring.scatter_sum([dkey_one, dvalue_one], order_b, 2 * rows)
    dnormed_one = to_owner(part_one, own)
    last = norm_back(
        own_rows(plain_one[:both], own), own_rows(inverse_one[:both], own), gain_one, dnormed_one
    )
    input_grad = own_rows(dhidden_one, own) + last

    def split(block, widths):
        cuts = [sum(widths[:i]) for i in range(len(widths) + 1)]
        return [block[:, cuts[i] : cuts[i + 1]] for i in range(len(widths))]

    def finished(block, widths):
        first, later = ring.unhalve(block)
        pieces = zip(split(first, widths), split(later, widths))
        return [jnp.concatenate(pair, axis=1) for pair in pieces]

    mlp_dgate = unit_whole(*ring.unhalve(mlp_dgate), units)
    mlp_dup = unit_whole(*ring.unhalve(mlp_dup), units)
    cross_dout, cross_dquery = finished(cross_a, [half] * 2)
    cross_dkey, cross_dvalue = finished(cross_b, [half] * 2)
    self_first, self_later = ring.unhalve(self_a)
    dgain_columns = self_first[:, 2 * half : 2 * half + 3] + self_later[:, 2 * half : 2 * half + 3]
    self_dquery = jnp.concatenate([self_first[:, :half], self_later[:, :half]], axis=1)
    self_dout = jnp.concatenate(
        [self_first[:, half : 2 * half], self_later[:, half : 2 * half]], axis=1
    )
    self_dkey, self_dvalue = finished(self_b, [half] * 2)

    return (
        output[None],
        input_grad[None],
        memory_grad[None],
        dgain_columns[:, 0],
        self_dquery,
        self_dkey,
        self_dvalue,
        self_dout,
        dgain_columns[:, 1],
        cross_dquery,
        cross_dkey,
        cross_dvalue,
        cross_dout,
        dgain_columns[:, 2],
        mlp_dgate,
        mlp_dup,
        mlp_ddown,
    )


def solution(mesh):
    rows = P(("dp", "head"), None)
    vector = P(("dp", "head"))
    grid = P("dp", "head", None)
    in_specs = (grid, grid, P("dp"), P("dp"))
    in_specs += (vector, rows, rows, rows, rows) * 2
    in_specs += (vector, rows, rows, rows, grid)
    out_specs = (grid, grid, grid)
    out_specs += (vector, rows, rows, rows, rows) * 2
    out_specs += (vector, rows, rows, rows)
    return jax.shard_map(
        on_device, mesh=mesh, in_specs=in_specs, out_specs=out_specs, check_vma=False
    )
```

time: 1880 us -> 551 us (0.29)
  waiting for transfers between devices: 1270 us -> 185 us
  blocking collectives: 140 us -> 0 us
  matrix products: 160 us -> 62.6 us
  local copies, waits for them, and re-layouts: 141 us -> 60 us
  Pallas kernels: 0 us -> 74 us
  starting transfers between devices: 42.3 us -> 92.7 us
  other arithmetic: 95.5 us -> 63.5 us
    reduce_scatter x9 -> x0, waiting for transfers between devices: 674 us -> none  [the longest x1 121 us: on_device(): lax.psum_scatter(mlp_dup, ('dp', 'head'), scatter_dimension=0, tiled=True)]
    all_gather x11 -> x0, waiting for transfers between devices: 426 us -> none  [the longest x1 56.3 us: on_device(): lax.all_gather(mlp_down, ('dp', 'head'), axis=0, tiled=True)]
    ppermute x0 -> x92, waiting for transfers between devices: none -> 185 us  [send(): return lax.ppermute(values, axis, [(i, i ^ bit) for i in range(size)])]
    unnamed x24 -> x0, waiting for transfers between devices: 143 us -> none
    dot_general x61 -> x33, matrix products: 160 us -> 62.6 us  [the longest x11 23.8 us: dot_nt(): return lax.dot_general(left, right, NT, preferred_element_type=F32)]
    ppermute x0 -> x92, starting transfers between devices: none -> 92.7 us  [send(): return lax.ppermute(values, axis, [(i, i ^ bit) for i in range(size)])]
    unnamed x2 -> x0, blocking collectives: 81.3 us -> none
    pallas_call x0 -> x20, Pallas kernels: none -> 74 us  [the longest x2 20.9 us: attention_backward(): pl.pallas_call(functools.partial(backward_kernel, causal, chunk), out_sha...]
  transfers between devices with their start and end apart: 33 -> 92, of which waited for: 23 -> 45; matrix products, arithmetic and copies ran while one was open for 19% -> 28% of each run, Pallas kernels for 0% -> 13%
where the time goes in v1:
time: 551 us; the launch traced here: 542 us
  waiting for transfers between devices  185 us (34%)
  starting transfers between devices  92.7 us (17%)
  Pallas kernels  74 us (13%)
  other arithmetic  63.5 us (12%)
  matrix products  62.6 us (11%)
  local copies, waits for them, and re-layouts  60 us (11%)
    ppermute x92, waiting for transfers between devices, send(): return lax.ppermute(values, axis, [(i, i ^ bit) for i in range(size)])  185 us
    ppermute x92, starting transfers between devices, send(): return lax.ppermute(values, axis, [(i, i ^ bit) for i in range(size)])  92.7 us
    unnamed x234, local copies, waits for them, and re-layouts  31.5 us
    dot_general x11, matrix products, dot_nt(): return lax.dot_general(left, right, NT, preferred_element_type=F32)  23.8 us
    dot_general x11, matrix products, dot_tn(): return lax.dot_general(left, right, TN, preferred_element_type=F32)  23.6 us
    pallas_call x2, Pallas kernels, attention_backward(): pl.pallas_call(functools.partial(backward_kernel, causal, chunk), out_sha...  20.9 us
    pallas_call x8, Pallas kernels, to_whole(): pl.pallas_call(functools.partial(whole_kernel, count, rows, cuts), out_sh...  19.4 us
    pallas_call x8, Pallas kernels, to_halves(): pl.pallas_call(functools.partial(halves_kernel, count, rows, cuts_of(widt...  19.4 us
  transfers between devices with their start and end apart: 92, of which 45 were waited for; matrix products, arithmetic and copies ran while one was open for 28% of the time, Pallas kernels for 13%

profile of v1, /device:TPU:0, one launch (start us, length us, event | category | flops | bytes accessed | tf_op | source)
XLA Modules:
  0.0 542.0 jit_solution(16383243343409719162)
XLA Ops:
  53.7 8.2 %collective-permute-done.4 = bf16[2,48,512]{2,1,0:T(8,128)(2,1)S(1)} collective-permute-done((bf16[2,48,512]{2,1,0:T(8,128)(2,1)S(1)}, bf16[2,48,512]{2,1,0:T(8,128)(2,1)S(1)}, u32[]{:S(2)}, u32[]{:S(2)}) %collective-permute-start.4) | collective-permute-done | bytes 98336 | tf_op jit(solution)/shard_map/ppermute | solution.py:324
  62.6 8.3 %collective-permute-done.23 = bf16[2,48,768]{2,1,0:T(8,128)(2,1)S(1)} collective-permute-done((bf16[2,48,768]{2,1,0:T(8,128)(2,1)S(1)}, bf16[2,48,768]{2,1,0:T(8,128)(2,1)S(1)}, u32[]{:S(2)}, u32[]{:S(2)}) %collective-permute-start.23) | collective-permute-done | bytes 147488 | tf_op jit(solution)/shard_map/ppermute | solution.py:324
  74.8 8.8 %collective-permute-done.30 = bf16[2,48,1024]{2,1,0:T(8,128)(2,1)S(1)} collective-permute-done((bf16[2,48,1024]{2,1,0:T(8,128)(2,1)S(1)}, bf16[2,48,1024]{2,1,0:T(8,128)(2,1)S(1)}, u32[]{:S(2)}, u32[]{:S(2)}) %collective-permute-start.30) | collective-permute-done | bytes 196640 | tf_op jit(solution)/shard_map/ppermute | solution.py:324
  119.2 11.3 %collective-permute-done.41 = bf16[8,64,384]{2,1,0:T(8,128)(2,1)S(1)} collective-permute-done((bf16[8,64,384]{2,1,0:T(8,128)(2,1)S(1)}, bf16[8,64,384]{2,1,0:T(8,128)(2,1)S(1)}, u32[]{:S(2)}, u32[]{:S(2)}) %collective-permute-start.41) | collective-permute-done | bytes 393248 | tf_op jit(solution)/shard_map/ppermute | solution.py:324
  157.7 8.2 %collective-permute-done.11 = bf16[8,48,768]{2,1,0:T(8,128)(2,1)} collective-permute-done((bf16[8,48,768]{2,1,0:T(8,128)(2,1)}, bf16[8,48,768]{2,1,0:T(8,128)(2,1)}, u32[]{:S(2)}, u32[]{:S(2)}) %collective-permute-start.11) | collective-permute-done | bytes 589856 | tf_op jit(solution)/shard_map/ppermute | solution.py:324
  179.5 5.8 %shard_map.388 = (bf16[512,384]{1,0:T(8,128)(2,1)S(1)}, f32[3,2,512]{2,1,0:T(2,128)S(1)}) custom-call(s32[6]{0:T(128)S(1)} %pad_add_fusion.info, bf16[512,384]{1,0:T(8,128)(2,1)S(1)} %convolution_convert_fusion.18.q_ref, bf16[1024,384]{1,0:T(8,128)(2,1)S(1)} %convolution_convert_fusion.6.k_ref, bf16[1024,384]{1,0:T(8,128)(2,1)S(1)} %convolution_convert_fusion.5.v_ref), custom_call_target="tpu_custom_call" | custom-call | flops 3221225472 | bytes 2359296 | tf_op jit(solution)/shard_map/pallas_call | solution.py:161
  185.3 7.0 %collective-permute-done.17 = bf16[8,48,1152]{2,1,0:T(8,128)(2,1)S(1)} collective-permute-done((bf16[8,48,1152]{2,1,0:T(8,128)(2,1)S(1)}, bf16[8,48,1152]{2,1,0:T(8,128)(2,1)S(1)}, u32[]{:S(2)}, u32[]{:S(2)}) %collective-permute-start.17) | collective-permute-done | bytes 884768 | tf_op jit(solution)/shard_map/ppermute | solution.py:324
  219.8 8.7 %shard_map.391 = (bf16[512,384]{1,0:T(8,128)(2,1)S(1)}, f32[3,2,512]{2,1,0:T(2,128)S(1)}) custom-call(s32[10]{0:T(128)S(1)} %pad_add_fusion.1.info, bf16[512,384]{1,0:T(8,128)(2,1)S(1)} %convolution_convert_fusion.17.q_ref, bf16[2048,384]{1,0:T(8,128)(2,1)S(1)} %convolution_convert_fusion.1.k_ref, bf16[2048,384]{1,0:T(8,128)(2,1)S(1)} %convolution_convert_fusion.v_ref), custom_call_target="tpu_custom_call" | custom-call | flops 6442450944 | bytes 3932160 | tf_op jit(solution)/shard_map/pallas_call | solution.py:161
  281.1 12.0 %collective-permute-done.85 = bf16[4,64,384]{2,1,0:T(8,128)(2,1)S(1)} collective-permute-done((bf16[4,64,384]{2,1,0:T(8,128)(2,1)S(1)}, bf16[4,64,384]{2,1,0:T(8,128)(2,1)S(1)}, u32[]{:S(2)}, u32[]{:S(2)}) %collective-permute-start.85) | collective-permute-done | bytes 196640 | tf_op jit(solution)/shard_map/ppermute | solution.py:324
  293.1 8.7 %collective-permute-start.86 = (bf16[2,64,384]{2,1,0:T(8,128)(2,1)S(1)}, bf16[2,64,384]{2,1,0:T(8,128)(2,1)S(1)}, u32[]{:S(2)}, u32[]{:S(2)}) collective-permute-start(bf16[2,64,384]{2,1,0:T(8,128)(2,1)S(1)} %get-tuple-element.153), channel_id=1, source_target_pairs={{0,16},{4,20},{8,24},{12,28},{16,0},{20,4},{24,8},{28,12},{1,17},{... | collective-permute-start | bytes 294920 | tf_op jit(solution)/shard_map/ppermute | solution.py:324
  316.7 12.2 %shard_map.396 = (bf16[512,384]{1,0:T(8,128)(2,1)S(1)}, bf16[2048,384]{1,0:T(8,128)(2,1)S(1)}, bf16[2048,384]{1,0:T(8,128)(2,1)S(1)}) custom-call(s32[10]{0:T(128)S(1)} %pad_add_fusion.1.info, bf16[512,384]{1,0:T(8,128)(2,1)S(1)} %convolution_convert_fusion.17.q_ref, bf16[2048,384]{1,0:T(8,128)(2,1)S(1)} %copy-done.7, bf16[2048,384]{1,0:T(8,128)(2,1)S(1)} %copy-done.5, ...), custom_call_target="tpu_custom_call" | custom-call | flops 16106127360 | bytes 7864320 | tf_op jit(solution)/shard_map/pallas_call | solution.py:192
  330.5 4.5 fusion.75
  348.9 4.5 convolution_convert_fusion.8.refs_0_
  357.9 4.9 convolution_add_fusion
  366.6 16.6 %collective-permute-start.81 = (bf16[2,48,1024]{2,1,0:T(8,128)(2,1)S(1)}, bf16[2,48,1024]{2,1,0:T(8,128)(2,1)S(1)}, u32[]{:S(2)}, u32[]{:S(2)}) collective-permute-start(bf16[2,48,1024]{2,1,0:T(8,128)(2,1)S(1)} %get-tuple-element.135), channel_id=1, source_target_pairs={{0,16},{4,20},{8,24},{12,28},{16,0},{20,4},{24,8},{28,12},{1,17},{... | collective-permute-start | bytes 589832 | tf_op jit(solution)/shard_map/ppermute | solution.py:324
  387.6 9.2 %collective-permute-done.81 = bf16[2,48,1024]{2,1,0:T(8,128)(2,1)S(1)} collective-permute-done((bf16[2,48,1024]{2,1,0:T(8,128)(2,1)S(1)}, bf16[2,48,1024]{2,1,0:T(8,128)(2,1)S(1)}, u32[]{:S(2)}, u32[]{:S(2)}) %collective-permute-start.81) | collective-permute-done | bytes 196640 | tf_op jit(solution)/shard_map/ppermute | solution.py:324
  401.0 4.8 collective-permute-done.82
  415.5 8.7 %shard_map.397 = (bf16[512,384]{1,0:T(8,128)(2,1)S(1)}, bf16[1024,384]{1,0:T(8,128)(2,1)S(1)}, bf16[1024,384]{1,0:T(8,128)(2,1)S(1)}) custom-call(s32[6]{0:T(128)S(1)} %pad_add_fusion.info, bf16[512,384]{1,0:T(8,128)(2,1)S(1)} %convolution_convert_fusion.18.q_ref, bf16[1024,384]{1,0:T(8,128)(2,1)S(1)} %copy-done.3, bf16[1024,384]{1,0:T(8,128)(2,1)S(1)} %copy-done.1, ...), custom_call_target="tpu_custom_call" | custom-call | flops 8053063680 | bytes 4718592 | tf_op jit(solution)/shard_map/pallas_call | solution.py:192
  461.4 8.0 %collective-permute-done.66 = bf16[2,48,768]{2,1,0:T(8,128)(2,1)S(1)} collective-permute-done((bf16[2,48,768]{2,1,0:T(8,128)(2,1)S(1)}, bf16[2,48,768]{2,1,0:T(8,128)(2,1)S(1)}, u32[]{:S(2)}, u32[]{:S(2)}) %collective-permute-start.66) | collective-permute-done | bytes 147488 | tf_op jit(solution)/shard_map/ppermute | solution.py:324
  469.4 9.3 %collective-permute-done.71 = bf16[2,48,768]{2,1,0:T(8,128)(2,1)S(1)} collective-permute-done((bf16[2,48,768]{2,1,0:T(8,128)(2,1)S(1)}, bf16[2,48,768]{2,1,0:T(8,128)(2,1)S(1)}, u32[]{:S(2)}, u32[]{:S(2)}) %collective-permute-start.71) | collective-permute-done | bytes 147488 | tf_op jit(solution)/shard_map/ppermute | solution.py:324
  478.7 4.3 collective-permute-done.67
  496.1 6.1 %collective-permute-done.60 = bf16[4,48,768]{2,1,0:T(8,128)(2,1)S(1)} collective-permute-done((bf16[4,48,768]{2,1,0:T(8,128)(2,1)S(1)}, bf16[4,48,768]{2,1,0:T(8,128)(2,1)S(1)}, u32[]{:S(2)}, u32[]{:S(2)}) %collective-permute-start.60) | collective-permute-done | bytes 294944 | tf_op jit(solution)/shard_map/ppermute | solution.py:324
  505.4 5.7 %collective-permute-done.61 = bf16[2,48,768]{2,1,0:T(8,128)(2,1)S(1)} collective-permute-done((bf16[2,48,768]{2,1,0:T(8,128)(2,1)S(1)}, bf16[2,48,768]{2,1,0:T(8,128)(2,1)S(1)}, u32[]{:S(2)}, u32[]{:S(2)}) %collective-permute-start.61) | collective-permute-done | bytes 147488 | tf_op jit(solution)/shard_map/ppermute | solution.py:324
  518.2 13.8 %collective-permute-done.51 = bf16[1,256,768]{2,1,0:T(8,128)(2,1)S(1)} collective-permute-done((bf16[1,256,768]{2,1,0:T(8,128)(2,1)S(1)}, bf16[1,256,768]{2,1,0:T(8,128)(2,1)S(1)}, u32[]{:S(2)}, u32[]{:S(2)}) %collective-permute-start.51) | collective-permute-done | bytes 393248 | tf_op jit(solution)/shard_map/ppermute | solution.py:324
  (654 shorter events, 338.0 us)
Async XLA Ops:
  4.5 147.9 %collective-permute-start.19 = (bf16[1,512,768]{2,1,0:T(8,128)(2,1)}, bf16[1,512,768]{2,1,0:T(8,128)(2,1)}, u32[]{:S(2)}, u32[]{:S(2)}) collective-permute-start(bf16[1,512,768]{2,1,0:T(8,128)(2,1)} %param.28), channel_id=1, source_target_pairs={{0,2},{1,3},{2,0},{3,1},{4,6},{5,7},{6,4},{7,5},{8,10},{9,11},{10,... | collective-permute-start | bytes 2359304 | tf_op jit(solution)/shard_map/ppermute | solution.py:324
  7.7 96.6 %collective-permute-start = (bf16[1,256,768]{2,1,0:T(8,128)(2,1)}, bf16[1,256,768]{2,1,0:T(8,128)(2,1)}, u32[]{:S(2)}, u32[]{:S(2)}) collective-permute-start(bf16[1,256,768]{2,1,0:T(8,128)(2,1)} %param.27), channel_id=1, source_target_pairs={{0,2},{1,3},{2,0},{3,1},{4,6},{5,7},{6,4},{7,5},{8,10},{9,11},{10,... | collective-permute-start | bytes 1179656 | tf_op jit(solution)/shard_map/ppermute | solution.py:324
  24.0 77.9 %collective-permute-start.47 = (bf16[256,768]{1,0:T(8,128)(2,1)S(1)}, bf16[256,768]{1,0:T(8,128)(2,1)S(1)}, u32[]{:S(2)}, u32[]{:S(2)}) collective-permute-start(bf16[256,768]{1,0:T(8,128)(2,1)S(1)} %bitcast.215), channel_id=1, source_target_pairs={{0,1},{1,0},{2,3},{3,2},{4,5},{5,4},{6,7},{7,6},{8,9},{9,8},{10,11... | collective-permute-start | bytes 1179656 | tf_op jit(solution)/shard_map/ppermute | solution.py:324
  133.2 37.1 %collective-permute-start.1 = (bf16[2,256,768]{2,1,0:T(8,128)(2,1)}, bf16[2,256,768]{2,1,0:T(8,128)(2,1)}, u32[]{:S(2)}, u32[]{:S(2)}) collective-permute-start(bf16[2,256,768]{2,1,0:T(8,128)(2,1)} %constant_dynamic-update-slice_fusion), channel_id=1, source_target_pairs={{0,1},{1,0},{2,3},{3,2},{4,5},{5,4},{6,7},{7,6},{8,9},{9,8},{10,11... | collective-permute-start | bytes 2359304 | tf_op jit(solution)/shard_map/ppermute | solution.py:324
  134.2 62.3 %collective-permute-start.25 = (bf16[8,48,768]{2,1,0:T(8,128)(2,1)}, bf16[8,48,768]{2,1,0:T(8,128)(2,1)}, u32[]{:S(2)}, u32[]{:S(2)}) collective-permute-start(bf16[8,48,768]{2,1,0:T(8,128)(2,1)} %pad_maximum_fusion.16), channel_id=1, source_target_pairs={{0,4},{4,0},{8,12},{12,8},{16,20},{20,16},{24,28},{28,24},{1,5},{5... | collective-permute-start | bytes 1769480 | tf_op jit(solution)/shard_map/ppermute | solution.py:324
  152.4 51.6 %collective-permute-start.32 = (bf16[8,48,1024]{2,1,0:T(8,128)(2,1)}, bf16[8,48,1024]{2,1,0:T(8,128)(2,1)}, u32[]{:S(2)}, u32[]{:S(2)}) collective-permute-start(bf16[8,48,1024]{2,1,0:T(8,128)(2,1)} %pad_maximum_fusion.12), channel_id=1, source_target_pairs={{0,2},{1,3},{2,0},{3,1},{4,6},{5,7},{6,4},{7,5},{8,10},{9,11},{10,... | collective-permute-start | bytes 2359304 | tf_op jit(solution)/shard_map/ppermute | solution.py:324
  156.0 72.5 %collective-permute-start.37 = (bf16[8,48,1024]{2,1,0:T(8,128)(2,1)}, bf16[8,48,1024]{2,1,0:T(8,128)(2,1)}, u32[]{:S(2)}, u32[]{:S(2)}) collective-permute-start(bf16[8,48,1024]{2,1,0:T(8,128)(2,1)} %pad_maximum_fusion.13), channel_id=1, source_target_pairs={{0,4},{4,0},{8,12},{12,8},{16,20},{20,16},{24,28},{28,24},{1,5},{5... | collective-permute-start | bytes 2359304 | tf_op jit(solution)/shard_map/ppermute | solution.py:324
  165.9 47.1 %collective-permute-start.20 = (bf16[2,512,768]{2,1,0:T(8,128)(2,1)}, bf16[2,512,768]{2,1,0:T(8,128)(2,1)}, u32[]{:S(2)}, u32[]{:S(2)}) collective-permute-start(bf16[2,512,768]{2,1,0:T(8,128)(2,1)} %constant_dynamic-update-slice_fusion.17), channel_id=1, source_target_pairs={{0,1},{1,0},{2,3},{3,2},{4,5},{5,4},{6,7},{7,6},{8,9},{9,8},{10,11... | collective-permute-start | bytes 4718600 | tf_op jit(solution)/shard_map/ppermute | solution.py:324
  263.8 71.2 %collective-permute-start.79 = (bf16[8,48,1024]{2,1,0:T(8,128)(2,1)}, bf16[8,48,1024]{2,1,0:T(8,128)(2,1)}, u32[]{:S(2)}, u32[]{:S(2)}) collective-permute-start(bf16[8,48,1024]{2,1,0:T(8,128)(2,1)} %get-tuple-element.82), channel_id=1, source_target_pairs={{0,4},{4,0},{8,12},{12,8},{16,20},{20,16},{24,28},{28,24},{1,5},{5... | collective-permute-start | bytes 2359304 | tf_op jit(solution)/shard_map/ppermute | solution.py:324
  271.6 72.9 %collective-permute-start.74 = (bf16[8,48,1024]{2,1,0:T(8,128)(2,1)}, bf16[8,48,1024]{2,1,0:T(8,128)(2,1)S(1)}, u32[]{:S(2)}, u32[]{:S(2)}) collective-permute-start(bf16[8,48,1024]{2,1,0:T(8,128)(2,1)} %get-tuple-element.80), channel_id=1, source_target_pairs={{0,2},{1,3},{2,0},{3,1},{4,6},{5,7},{6,4},{7,5},{8,10},{9,11},{10,... | collective-permute-start | bytes 2359304 | tf_op jit(solution)/shard_map/ppermute | solution.py:324
  275.0 37.4 %collective-permute-start.48 = (bf16[512,768]{1,0:T(8,128)(2,1)S(1)}, bf16[512,768]{1,0:T(8,128)(2,1)S(1)}, u32[]{:S(2)}, u32[]{:S(2)}) collective-permute-start(bf16[512,768]{1,0:T(8,128)(2,1)S(1)} %get-tuple-element.230), channel_id=1, source_target_pairs={{0,1},{1,0},{2,3},{3,2},{4,5},{5,4},{6,7},{7,6},{8,9},{9,8},{10,11... | collective-permute-start | bytes 2359304 | tf_op jit(solution)/shard_map/ppermute | solution.py:324
  348.2 36.3 %collective-permute-start.64 = (bf16[8,48,768]{2,1,0:T(8,128)(2,1)}, bf16[8,48,768]{2,1,0:T(8,128)(2,1)}, u32[]{:S(2)}, u32[]{:S(2)}) collective-permute-start(bf16[8,48,768]{2,1,0:T(8,128)(2,1)} %get-tuple-element.76), channel_id=1, source_target_pairs={{0,2},{1,3},{2,0},{3,1},{4,6},{5,7},{6,4},{7,5},{8,10},{9,11},{10,... | collective-permute-start | bytes 1769480 | tf_op jit(solution)/shard_map/ppermute | solution.py:324
  355.9 30.7 %collective-permute-start.69 = (bf16[8,48,768]{2,1,0:T(8,128)(2,1)}, bf16[8,48,768]{2,1,0:T(8,128)(2,1)S(1)}, u32[]{:S(2)}, u32[]{:S(2)}) collective-permute-start(bf16[8,48,768]{2,1,0:T(8,128)(2,1)} %get-tuple-element.78), channel_id=1, source_target_pairs={{0,4},{4,0},{8,12},{12,8},{16,20},{20,16},{24,28},{28,24},{1,5},{5... | collective-permute-start | bytes 1769480 | tf_op jit(solution)/shard_map/ppermute | solution.py:324
  357.9 52.5 %collective-permute-start.49 = (bf16[512,768]{1,0:T(8,128)(2,1)S(1)}, bf16[512,768]{1,0:T(8,128)(2,1)S(1)}, u32[]{:S(2)}, u32[]{:S(2)}) collective-permute-start(bf16[512,768]{1,0:T(8,128)(2,1)S(1)} %get-tuple-element.232), channel_id=1, source_target_pairs={{0,1},{1,0},{2,3},{3,2},{4,5},{5,4},{6,7},{7,6},{8,9},{9,8},{10,11... | collective-permute-start | bytes 2359304 | tf_op jit(solution)/shard_map/ppermute | solution.py:324
  364.4 138.4 %collective-permute-start.52 = (bf16[2,512,768]{2,1,0:T(8,128)(2,1)}, bf16[2,512,768]{2,1,0:T(8,128)(2,1)}, u32[]{:S(2)}, u32[]{:S(2)}) collective-permute-start(bf16[2,512,768]{2,1,0:T(8,128)(2,1)} %fusion.7), channel_id=1, source_target_pairs={{0,1},{1,0},{2,3},{3,2},{4,5},{5,4},{6,7},{7,6},{8,9},{9,8},{10,11... | collective-permute-start | bytes 4718600 | tf_op jit(solution)/shard_map/ppermute | solution.py:324
  366.6 30.2 %collective-permute-start.81 = (bf16[2,48,1024]{2,1,0:T(8,128)(2,1)S(1)}, bf16[2,48,1024]{2,1,0:T(8,128)(2,1)S(1)}, u32[]{:S(2)}, u32[]{:S(2)}) collective-permute-start(bf16[2,48,1024]{2,1,0:T(8,128)(2,1)S(1)} %get-tuple-element.135), channel_id=1, source_target_pairs={{0,16},{4,20},{8,24},{12,28},{16,0},{20,4},{24,8},{28,12},{1,17},{... | collective-permute-start | bytes 589832 | tf_op jit(solution)/shard_map/ppermute | solution.py:324
  386.6 71.3 %collective-permute-start.65 = (bf16[4,48,768]{2,1,0:T(8,128)(2,1)}, bf16[4,48,768]{2,1,0:T(8,128)(2,1)}, u32[]{:S(2)}, u32[]{:S(2)}) collective-permute-start(bf16[4,48,768]{2,1,0:T(8,128)(2,1)} %get-tuple-element.123), channel_id=1, source_target_pairs={{0,4},{4,0},{8,12},{12,8},{16,20},{20,16},{24,28},{28,24},{1,5},{5... | collective-permute-start | bytes 884744 | tf_op jit(solution)/shard_map/ppermute | solution.py:324
  396.8 62.3 %collective-permute-start.70 = (bf16[4,48,768]{2,1,0:T(8,128)(2,1)}, bf16[4,48,768]{2,1,0:T(8,128)(2,1)}, u32[]{:S(2)}, u32[]{:S(2)}) collective-permute-start(bf16[4,48,768]{2,1,0:T(8,128)(2,1)} %get-tuple-element.121), channel_id=1, source_target_pairs={{0,2},{1,3},{2,0},{3,1},{4,6},{5,7},{6,4},{7,5},{8,10},{9,11},{10,... | collective-permute-start | bytes 884744 | tf_op jit(solution)/shard_map/ppermute | solution.py:324
  410.4 37.2 %collective-permute-start.83 = (f32[24,1024]{1,0:T(8,128)S(1)}, f32[24,1024]{1,0:T(8,128)S(1)}, u32[]{:S(2)}, u32[]{:S(2)}) collective-permute-start(f32[24,1024]{1,0:T(8,128)S(1)} %select_bitcast_fusion), channel_id=1, source_target_pairs={{0,1},{1,0},{2,3},{3,2},{4,5},{5,4},{6,7},{7,6},{8,9},{9,8},{10,11... | collective-permute-start | bytes 294920 | tf_op jit(solution)/shard_map/ppermute | solution.py:324
  410.5 41.3 %collective-permute-start.78 = (f32[24,1024]{1,0:T(8,128)S(1)}, f32[24,1024]{1,0:T(8,128)S(1)}, u32[]{:S(2)}, u32[]{:S(2)}) collective-permute-start(f32[24,1024]{1,0:T(8,128)S(1)} %select_bitcast_fusion.1), channel_id=1, source_target_pairs={{0,1},{1,0},{2,3},{3,2},{4,5},{5,4},{6,7},{7,6},{8,9},{9,8},{10,11... | collective-permute-start | bytes 294920 | tf_op jit(solution)/shard_map/ppermute | solution.py:324
  447.6 46.2 %collective-permute-start.54 = (bf16[8,48,896]{2,1,0:T(8,128)(2,1)}, bf16[8,48,896]{2,1,0:T(8,128)(2,1)}, u32[]{:S(2)}, u32[]{:S(2)}) collective-permute-start(bf16[8,48,896]{2,1,0:T(8,128)(2,1)} %get-tuple-element.72), channel_id=1, source_target_pairs={{0,2},{1,3},{2,0},{3,1},{4,6},{5,7},{6,4},{7,5},{8,10},{9,11},{10,... | collective-permute-start | bytes 2064392 | tf_op jit(solution)/shard_map/ppermute | solution.py:324
  451.8 40.1 %collective-permute-start.59 = (bf16[8,48,768]{2,1,0:T(8,128)(2,1)}, bf16[8,48,768]{2,1,0:T(8,128)(2,1)}, u32[]{:S(2)}, u32[]{:S(2)}) collective-permute-start(bf16[8,48,768]{2,1,0:T(8,128)(2,1)} %get-tuple-element.74), channel_id=1, source_target_pairs={{0,4},{4,0},{8,12},{12,8},{16,20},{20,16},{24,28},{28,24},{1,5},{5... | collective-permute-start | bytes 1769480 | tf_op jit(solution)/shard_map/ppermute | solution.py:324
  457.9 53.3 %collective-permute-start.50 = (bf16[2,256,768]{2,1,0:T(8,128)(2,1)}, bf16[2,256,768]{2,1,0:T(8,128)(2,1)S(1)}, u32[]{:S(2)}, u32[]{:S(2)}) collective-permute-start(bf16[2,256,768]{2,1,0:T(8,128)(2,1)} %fusion.11), channel_id=1, source_target_pairs={{0,1},{1,0},{2,3},{3,2},{4,5},{5,4},{6,7},{7,6},{8,9},{9,8},{10,11... | collective-permute-start | bytes 2359304 | tf_op jit(solution)/shard_map/ppermute | solution.py:324
  505.0 35.3 %collective-permute-start.53 = (bf16[1,512,768]{2,1,0:T(8,128)(2,1)S(1)}, bf16[1,512,768]{2,1,0:T(8,128)(2,1)S(1)}, u32[]{:S(2)}, u32[]{:S(2)}) collective-permute-start(bf16[1,512,768]{2,1,0:T(8,128)(2,1)S(1)} %slice.1070), channel_id=1, source_target_pairs={{0,2},{1,3},{2,0},{3,1},{4,6},{5,7},{6,4},{7,5},{8,10},{9,11},{10,... | collective-permute-start | bytes 2359304 | tf_op jit(solution)/shard_map/ppermute | solution.py:324
  (172 other events, 1470.6 us)

commit v2 on v1

--- a/solution.py
+++ b/solution.py
@@ -6,6 +6,7 @@
 from jax import lax
 from jax.experimental import pallas as pl
 from jax.experimental.pallas import tpu as pltpu
+from jax.sharding import Mesh
 from jax.sharding import PartitionSpec as P
 
 HEAD_DIM = 64
@@ -219,11 +220,23 @@
     )(info, queries, keys, values, context, grads, lse)
 
 
-def whole_kernel(count, rows, cuts, index, source, *targets):
+def whole_kernel(count, rows, cuts, index, first, later, *targets):
+    half = count // 2
     for step in range(count):
         at = index[step]
-        for cut, target in zip(cuts, targets):
-            target[pl.ds(step * rows, rows), :] = source[at, :, pl.ds(cut, target.shape[1])]
+        place = pl.ds(step * rows, rows)
+
+        def put(source, block):
+            for cut, target in zip(cuts, targets):
+                target[place, :] = source[block, :, pl.ds(cut, target.shape[1])]
+
+        @pl.when(at < half)
+        def _():
+            put(first, at)
+
+        @pl.when(at >= half)
+        def _():
+            put(later, at - half)
 
 
 def halves_kernel(count, rows, cuts, index, *refs):
@@ -243,21 +256,23 @@
     return [pl.BlockSpec(memory_space=pltpu.VMEM)] * number
 
 
-def to_whole(blocks, index, widths):
-    count, rows, columns = blocks.shape
+def to_whole(first, later, index, widths):
+    half, rows, columns = first.shape
+    count = 2 * half
     cuts = cuts_of(widths)
     if rows % 16:
+        blocks = jnp.concatenate([first, later], axis=0)
         whole = jnp.take(blocks, index, axis=0).reshape(count * rows, columns)
         return [whole[:, cut : cut + width] for cut, width in zip(cuts, widths)]
     return pl.pallas_call(
         functools.partial(whole_kernel, count, rows, cuts),
-        out_shape=[jax.ShapeDtypeStruct((count * rows, width), blocks.dtype) for width in widths],
-        in_specs=[pl.BlockSpec(memory_space=pltpu.SMEM)] + vmem_specs(1),
+        out_shape=[jax.ShapeDtypeStruct((count * rows, width), first.dtype) for width in widths],
+        in_specs=[pl.BlockSpec(memory_space=pltpu.SMEM)] + vmem_specs(2),
         out_specs=vmem_specs(len(widths)),
         cost_estimate=pl.CostEstimate(
             flops=0, transcendentals=0, bytes_accessed=4 * count * rows * columns
         ),
-    )(index, blocks)
+    )(index, first, later)
 
 
 def to_halves(wholes, index, rows):
@@ -281,6 +296,190 @@
     )(index, *wholes)
 
 
+def unit_tile(source, at, second):
+    lanes = 2 * HEAD_DIM
+    start = 2 * at * lanes + (HEAD_DIM if second else 0)
+    return jnp.concatenate(
+        [source[:, pl.ds(start, HEAD_DIM)], source[:, pl.ds(start + lanes, HEAD_DIM)]], axis=1
+    )
+
+
+def shards_kernel(kinds, place, *refs):
+    sources, targets = refs[:-2], refs[-2:]
+
+    def write(target, second):
+        cut = 0
+        for kind, source in zip(kinds, sources):
+            columns = source.shape[1]
+            if kind == "all":
+                target[:, pl.ds(cut, columns)] = source[...]
+                cut += columns
+                continue
+            if kind == "half":
+                start = columns // 2 if second else 0
+                target[:, pl.ds(cut, columns // 2)] = source[:, pl.ds(start, columns // 2)]
+            else:
+                for tile in range(columns // 256):
+                    target[:, pl.ds(cut + 128 * tile, 128)] = unit_tile(source, tile, second)
+            cut += columns // 2
+
+    @pl.when(place[0] == 0)
+    def _():
+        write(targets[0], False)
+        write(targets[1], True)
+
+    @pl.when(place[0] != 0)
+    def _():
+        write(targets[0], True)
+        write(targets[1], False)
+
+
+def rows_kernel(widths, piece, place, mine, other, down, *targets):
+    rows = mine.shape[0]
+
+    def write(upper, lower):
+        cut = 0
+        for target, width in zip(targets[:-1], widths):
+            target[0, pl.ds(0, rows), :] = upper[:, pl.ds(cut, width)]
+            target[0, pl.ds(rows, rows), :] = lower[:, pl.ds(cut, width)]
+            cut += width
+        packed = targets[-1]
+        columns = (mine.shape[1] - cut) // 2
+        step = 8
+        for start in range(0, 2 * rows, step):
+            source = upper if start < rows else lower
+            number, inner = start // piece, start % piece
+            for matrix in range(2):
+                place_at = (matrix * (2 * rows // piece) + number) * columns
+                packed[pl.ds(inner, step), pl.ds(place_at, columns)] = source[
+                    pl.ds(start % rows, step), pl.ds(cut + matrix * columns, columns)
+                ]
+        base = 2 * (2 * rows // piece) * columns
+        width = down.shape[1]
+        for number in range(down.shape[0] // piece):
+            packed[:, pl.ds(base + number * width, width)] = down[pl.ds(number * piece, piece), :]
+
+    @pl.when(place[0] == 0)
+    def _():
+        write(mine, other)
+
+    @pl.when(place[0] != 0)
+    def _():
+        write(other, mine)
+
+
+SMEM_SPEC = pl.BlockSpec(memory_space=pltpu.SMEM)
+
+
+def cut_shards(place, shards, kinds):
+    rows = shards[0].shape[0]
+    columns = sum(w.shape[1] if k == "all" else w.shape[1] // 2 for w, k in zip(shards, kinds))
+    shape = jax.ShapeDtypeStruct((rows, columns), LOW)
+    return pl.pallas_call(
+        functools.partial(shards_kernel, kinds),
+        out_shape=[shape, shape],
+        in_specs=[SMEM_SPEC] + vmem_specs(len(shards)),
+        out_specs=vmem_specs(2),
+    )(place, *shards)
+
+
+def join_rows(place, mine, other, down, widths, piece):
+    rows = 2 * mine.shape[0]
+    rest = mine.shape[1] - sum(widths)
+    packed = rest * (rows // piece) + down.shape[1] * (down.shape[0] // piece)
+    return pl.pallas_call(
+        functools.partial(rows_kernel, widths, piece),
+        out_shape=[jax.ShapeDtypeStruct((1, rows, width), LOW) for width in widths]
+        + [jax.ShapeDtypeStruct((piece, packed), LOW)],
+        in_specs=[SMEM_SPEC] + vmem_specs(3),
+        out_specs=vmem_specs(len(widths) + 1),
+    )(place, mine, other, down)
+
+
+def mlp_kernel(
+    chunk, a_ref, g_ref, w_ref, part_ref, down_ref, grad_ref, gate_w, up_w, down_w, p_acc, d_acc, sems
+):
+    blocks, pieces, piece, units = gate_w.shape
+    down_pieces, width = down_w.shape[1], down_w.shape[3]
+    moves = []
+    for number in range(pieces):
+        moves.append((w_ref.at[:, :, pl.ds(number * units, units)], gate_w.at[:, number]))
+    for number in range(pieces):
+        moves.append((w_ref.at[:, :, pl.ds((pieces + number) * units, units)], up_w.at[:, number]))
+    base = 2 * pieces * units
+    for number in range(down_pieces):
+        moves.append((w_ref.at[:, :, pl.ds(base + number * width, width)], down_w.at[:, number]))
+    copies = [pltpu.make_async_copy(a, b, sems.at[i]) for i, (a, b) in enumerate(moves)]
+    for copy in copies:
+        copy.start()
+    for copy in copies:
+        copy.wait()
+
+    a_in = a_ref[...]
+    g_in = g_ref[...]
+    per_block = down_pieces * piece
+    step_blocks = chunk // per_block
+    for start in range(0, units, chunk):
+        columns = pl.ds(start, chunk)
+        gate_part = gate_w[:, :, :, columns].reshape(blocks * pieces * piece, chunk)
+        up_part = up_w[:, :, :, columns].reshape(blocks * pieces * piece, chunk)
+        block_at = start // per_block
+        down_part = down_w[pl.ds(block_at, step_blocks)].reshape(chunk, width)
+        gate = dot_nn(a_in, gate_part)
+        up = dot_nn(a_in, up_part)
+        active, slope = gelu_parts(gate)
+        mixed = (active * up).astype(LOW)
+        grad = dot_nt(g_in, down_part)
+        gate_low = (grad * up * slope).astype(LOW)
+        up_low = (grad * active).astype(LOW)
+        down_new = dot_nn(mixed, down_part)
+        part_new = dot_nt(gate_low, gate_part) + dot_nt(up_low, up_part)
+        if start == 0:
+            d_acc[...] = down_new
+            p_acc[...] = part_new
+        else:
+            d_acc[...] += down_new
+            p_acc[...] += part_new
+        dgate = dot_tn(a_in, gate_low).astype(LOW).reshape(blocks, pieces, piece, chunk)
+        dup = dot_tn(a_in, up_low).astype(LOW).reshape(blocks, pieces, piece, chunk)
+        for number in range(pieces):
+            grad_ref[:, :, pl.ds(number * units + start, chunk)] = dgate[:, number]
+            grad_ref[:, :, pl.ds((pieces + number) * units + start, chunk)] = dup[:, number]
+        ddown = dot_tn(mixed, g_in).astype(LOW).reshape(step_blocks, down_pieces, piece, width)
+        for number in range(down_pieces):
+            grad_ref[pl.ds(block_at, step_blocks), :, pl.ds(base + number * width, width)] = ddown[
+                :, number
+            ]
+    part_ref[...] = p_acc[...]
+    down_ref[...] = d_acc[...]
+
+
+def feed_forward(normed, grads, packed, pieces, down_pieces, units):
+    rows, width = normed.shape
+    blocks, piece, columns = packed.shape
+    big = jax.ShapeDtypeStruct((rows, width), F32)
+    return pl.pallas_call(
+        functools.partial(mlp_kernel, 256),
+        out_shape=[big, big, jax.ShapeDtypeStruct(packed.shape, LOW)],
+        in_specs=vmem_specs(2) + [pl.BlockSpec(memory_space=pl.ANY)],
+        out_specs=vmem_specs(3),
+        scratch_shapes=[
+            pltpu.VMEM((blocks, pieces, piece, units), LOW),
+            pltpu.VMEM((blocks, pieces, piece, units), LOW),
+            pltpu.VMEM((blocks, down_pieces, piece, width), LOW),
+            pltpu.VMEM((rows, width), F32),
+            pltpu.VMEM((rows, width), F32),
+            pltpu.SemaphoreType.DMA((2 * pieces + down_pieces,)),
+        ],
+        compiler_params=pltpu.CompilerParams(vmem_limit_bytes=48 << 20),
+        cost_estimate=pl.CostEstimate(
+            flops=18 * rows * width * units,
+            transcendentals=rows * units,
+            bytes_accessed=4 * blocks * piece * columns + 12 * rows * width,
+        ),
+    )(normed, grads, packed)
+
+
 def normalize(values):
     inverse = lax.rsqrt(jnp.mean(values * values, axis=-1, keepdims=True) + EPS)
     return values * inverse, inverse
@@ -303,28 +502,26 @@
 
 class Ring:
     def __init__(self):
-        self.heads = lax.axis_size("head")
         self.charts = lax.axis_size("dp")
-        self.groups = self.heads // 2
-        place = lax.axis_index("head")
-        self.second = (place % 2) == 1
-        self.half = place % 2
-        self.group = place // 2
+        self.groups = lax.axis_size("hx")
+        self.half = lax.axis_index("hc")
+        self.second = self.half == 1
+        self.group = lax.axis_index("hx")
         self.block = lax.axis_index("dp") * self.groups + self.group
         self.blocks = self.charts * self.groups
         chart_bits = [("dp", 1 << i) for i in range(self.charts.bit_length() - 1)]
-        group_bits = [("head", 2 << i) for i in range(self.groups.bit_length() - 1)]
-        far = chart_bits[1:]
+        self.group_bits = [("hx", 1 << i) for i in range(self.groups.bit_length() - 1)]
+        self.far = chart_bits[1:]
         near = chart_bits[:1]
-        self.group_bits = group_bits
-        self.orders = (far + near + group_bits, far + group_bits + near)
+        self.tails = (near + self.group_bits, self.group_bits + near)
+        self.orders = tuple(self.far + tail for tail in self.tails)
 
     def send(self, values, axis, bit):
-        size = self.charts if axis == "dp" else self.heads
+        size = self.charts if axis == "dp" else self.groups
         return lax.ppermute(values, axis, [(i, i ^ bit) for i in range(size)])
 
     def swap(self, values):
-        return self.send(values, "head", 1)
+        return lax.ppermute(values, "hc", [(0, 1), (1, 0)])
 
     def in_order(self, mine, other):
         return jnp.where(self.second, other, mine), jnp.where(self.second, mine, other)
@@ -335,7 +532,7 @@
     def masks(self, order):
         masks = [0]
         for axis, bit in order:
-            step = bit * self.groups if axis == "dp" else bit // 2
+            step = bit * self.groups if axis == "dp" else bit
             masks = masks + [m ^ step for m in masks]
         return masks
 
@@ -343,30 +540,57 @@
         apart = self.block ^ jnp.arange(self.blocks, dtype=jnp.int32)
         index = jnp.zeros((self.blocks,), jnp.int32)
         for place, (axis, bit) in enumerate(order):
-            step = bit * self.groups if axis == "dp" else bit // 2
+            step = bit * self.groups if axis == "dp" else bit
             index = index + jnp.where((apart & step) != 0, 1 << place, 0)
         return index
 
     def origins(self, order):
         return self.block ^ jnp.asarray(self.masks(order), jnp.int32)
 
-    def gather(self, shard, order, widths):
-        blocks = shard[None]
-        for axis, bit in order:
+    def gather(self, blocks, widths):
+        for axis, bit in self.far:
             blocks = jnp.concatenate([blocks, self.send(blocks, axis, bit)], axis=0)
-        return to_whole(blocks, self.arrivals(order), widths)
-
-    def scatter_sum(self, wholes, order, rows):
-        keep, give = to_halves(wholes, self.origins(order), rows)
-        for place, (axis, bit) in enumerate(reversed(order)):
+        cut = sum(widths[0])
+        parts = [blocks[:, :, :cut], blocks[:, :, cut:]]
+        got = [None, None]
+        for place in range(len(self.tails[0])):
+            for side, tail in enumerate(self.tails):
+                if place:
+                    parts[side] = jnp.concatenate([parts[side], got[side]], axis=0)
+                got[side] = self.send(parts[side], *tail[place])
+        whole = []
+        for side, order in enumerate(self.orders):
+            whole += to_whole(parts[side], got[side], self.arrivals(order), widths[side])
+        return whole
+
+    def scatter_sum(self, sides, rows):
+        add = lambda keep, got: keep.astype(F32) + got.astype(F32)
+        keeps, gives = [], []
+        for wholes, order in zip(sides, self.orders):
+            keep, give = to_halves(wholes, self.origins(order), rows)
+            keeps.append(keep)
+            gives.append(give)
+        steps = len(self.tails[0])
+        for place in reversed(range(steps)):
+            for side, tail in enumerate(self.tails):
+                got = self.send(gives[side], *tail[place])
+                half = got.shape[0] // 2
+                if place:
+                    gives[side] = add(keeps[side][half:], got[half:]).astype(LOW)
+                    keeps[side] = add(keeps[side][:half], got[:half]).astype(LOW)
+                else:
+                    gives[side] = add(keeps[side][half:], got[half:])
+                    keeps[side] = add(keeps[side][:half], got[:half])
+        keep = jnp.concatenate(keeps, axis=2)
+        give = jnp.concatenate(gives, axis=2).astype(LOW)
+        for place, (axis, bit) in enumerate(reversed(self.far)):
             got = self.send(give, axis, bit)
             half = keep.shape[0] // 2
-            add = lambda cut: keep[cut].astype(F32) + got[cut].astype(F32)
             if half:
-                give = add(slice(half, None)).astype(LOW)
-                keep = add(slice(0, half)).astype(LOW)
+                give = add(keep[half:], got[half:]).astype(LOW)
+                keep = add(keep[:half], got[:half])
             else:
-                keep = add(slice(None))
+                keep = add(keep, got)
         return keep[0]
 
     def pair_rows(self, mine, axis=0):
@@ -432,7 +656,6 @@
     output_grad,
 ):
     ring = Ring()
-    order_a, order_b = ring.orders
     width = tokens.shape[-1]
     half = width // 2
     units = mlp_down.shape[0]
@@ -441,30 +664,45 @@
     own = tokens.shape[1]
     own_patches = memory.shape[1]
     both = 2 * own
+    piece = 16
+    packed = (2 * rows) % piece == 0 and units == HEAD_DIM and ring.blocks > 1
+    pieces, down_pieces = 2 * rows // piece, units // piece
+    pairs = ("dp", "hx")
 
     gain_columns = jnp.stack([self_gain, cross_gain, mlp_gain], axis=1)
     gain_columns = jnp.pad(gain_columns, ((0, 0), (0, PAIR_LANES - 3)))
-    first_a = ring.halves([column_halves(self_query), (gain_columns, gain_columns)])
-    first_b = ring.halves([column_halves(self_key), column_halves(self_value)])
+    group_one = [self_query, gain_columns, self_key, self_value]
+    group_two = [self_out, cross_query, cross_out, cross_key, cross_value]
+    kinds_one = ["half", "all", "half", "half"]
+    widths_one = ([half, PAIR_LANES], [half, half])
+    widths_two = ([half] * 3, [half] * 2)
+    total_one, total_two = 3 * half + PAIR_LANES, 5 * half
+    if packed:
+        place = ring.half.astype(jnp.int32)[None]
+        shards = group_one + group_two + [mlp_gate, mlp_up]
+        kinds = kinds_one + ["half"] * 5 + ["units"] * 2
+        mine, give = cut_shards(place, shards, kinds)
+        other = ring.swap(give)
+        blocks_one, blocks_two, blocks_mlp = join_rows(
+            place, mine, other, mlp_down, [total_one, total_two], piece
+        )
+        mlp_weights = lax.all_gather(blocks_mlp, pairs, axis=0, tiled=True)
+        mlp_weights = mlp_weights.reshape(ring.blocks, piece, -1)
+    else:
+        both_halves = lambda w, k: (w, w) if k == "all" else column_halves(w)
+        blocks_one = ring.halves([both_halves(w, k) for w, k in zip(group_one, kinds_one)])[None]
+        blocks_two = ring.halves([column_halves(w) for w in group_two])[None]
+        gate_up = ring.halves([unit_halves(mlp_gate, units), unit_halves(mlp_up, units)])
+        gate_up = lax.all_gather(gate_up, pairs, axis=0, tiled=True)
+        down_three = lax.all_gather(mlp_down, pairs, axis=0, tiled=True)
     token_rows = ring.pair_rows(ring.across(tokens[0]), 1).reshape(-1, width)
-    query_one, gains = ring.gather(first_a, order_a, [half, PAIR_LANES])
-    key_one, value_one = ring.gather(first_b, order_b, [half, half])
+    query_one, gains, key_one, value_one = ring.gather(blocks_one, widths_one)
     patch_rows = ring.pair_rows(ring.across(memory[0]), 1).reshape(-1, width)
-    next_a = ring.halves(
-        [column_halves(self_out), column_halves(cross_query), column_halves(cross_out)]
-    )
-    next_b = ring.halves([column_halves(cross_key), column_halves(cross_value)])
-    out_one_half, query_two, out_two_half = ring.gather(next_a, order_a, [half] * 3)
-    key_two, value_two = ring.gather(next_b, order_b, [half] * 2)
+    out_one_half, query_two, out_two_half, key_two, value_two = ring.gather(
+        blocks_two, widths_two
+    )
     out_one = ring.pair_rows(out_one_half, 1)
     out_two = ring.pair_rows(out_two_half, 1)
-    gate_rows = ring.halves([unit_halves(mlp_gate, units)])
-    up_rows = ring.halves([unit_halves(mlp_up, units)])
-    (gate_three,) = ring.gather(gate_rows, order_a, [hidden_half])
-    (up_three,) = ring.gather(up_rows, order_b, [hidden_half])
-    (down_left,) = ring.gather(mlp_down[:, :half], order_a, [half])
-    (down_right,) = ring.gather(mlp_down[:, half:], order_b, [half])
-    down_three = jnp.concatenate([down_left, down_right], axis=1)
     grad_low = ring.pair_rows(output_grad[0])
 
     gain_rows = gains[:, :3].astype(F32).T
@@ -508,42 +746,58 @@
     hidden_two = hidden_one + dot_nn(context_two, out_two)
     plain_three, inverse_three = normalize(hidden_two)
     normed_three = (plain_three * gain_three).astype(LOW)
-    gate = dot_nn(normed_three, gate_three)
-    up = dot_nn(normed_three, up_three)
-    active, slope = gelu_parts(gate)
-    mixed = (active * up).astype(LOW)
-
     def own_rows(values, count):
         return lax.dynamic_slice_in_dim(values, ring.half * count, count, 0)
 
     def other_rows(values, count):
         return lax.dynamic_slice_in_dim(values, (1 - ring.half) * count, count, 0)
 
-    down_part = dot_nn(mixed, down_three)
+    if packed:
+        part_three, down_part, mlp_terms = feed_forward(
+            normed_three, grad_low, mlp_weights, pieces, down_pieces, hidden_half
+        )
+        mlp_terms = mlp_terms.reshape(ring.blocks * piece, -1)
+        mlp_sum = lax.psum_scatter(mlp_terms, pairs, scatter_dimension=0, tiled=True)
+        mlp_sum = mlp_sum.astype(F32)
+        take = lambda at, size: mlp_sum[:, at : at + size]
+        gate_up = [
+            jnp.concatenate(
+                [take((m * pieces + j) * hidden_half, hidden_half) for j in range(pieces)], axis=0
+            )
+            for m in range(2)
+        ]
+        gate_up = jnp.concatenate(gate_up, axis=1)
+        base = 2 * pieces * hidden_half
+        mlp_ddown = jnp.concatenate(
+            [take(base + j * width, width) for j in range(down_pieces)], axis=0
+        )
+    else:
+        gate_three, up_three = gate_up[:, :hidden_half], gate_up[:, hidden_half:]
+        active, slope = gelu_parts(dot_nn(normed_three, gate_three))
+        up = dot_nn(normed_three, up_three)
+        mixed = (active * up).astype(LOW)
+        down_part = dot_nn(mixed, down_three)
+        grad_mixed = dot_nt(grad_low, down_three)
+        gate_low = (grad_mixed * up * slope).astype(LOW)
+        up_low = (grad_mixed * active).astype(LOW)
+        part_three = dot_nt(gate_low, gate_three) + dot_nt(up_low, up_three)
+        terms = jnp.concatenate(
+            [dot_tn(normed_three, gate_low), dot_tn(normed_three, up_low)], axis=1
+        )
+        gate_up = lax.psum_scatter(terms, pairs, scatter_dimension=0, tiled=True)
+        ddown = dot_tn(mixed, grad_low)
+        mlp_ddown = lax.psum_scatter(ddown, pairs, scatter_dimension=0, tiled=True)
+
     down_got = ring.swap(other_rows(down_part, own).astype(LOW))
     output = (
         own_rows(hidden_two, own) + own_rows(down_part, own) + down_got.astype(F32)
     ).astype(LOW)
-
     grad_float = grad_low.astype(F32)
-    ddown = dot_tn(mixed, grad_low).astype(LOW)
-    grad_mixed = dot_nt(grad_low, down_three)
-    gate_low = (grad_mixed * up * slope).astype(LOW)
-    up_low = (grad_mixed * active).astype(LOW)
-    dgate = dot_tn(normed_three, gate_low).astype(LOW)
-    dup = dot_tn(normed_three, up_low).astype(LOW)
-    part_three = dot_nt(gate_low, gate_three) + dot_nt(up_low, up_three)
     mlp_dgain = jnp.sum(part_three * plain_three, axis=0)
     part_low = part_three.astype(LOW)
     dnormed_three = part_low.astype(F32) + ring.swap(part_low).astype(F32)
     dhidden_two = grad_float + norm_back(plain_three, inverse_three, gain_three, dnormed_three)
     branch_two = dhidden_two.astype(LOW)
-    mlp_dgate = ring.scatter_sum([dgate], order_a, 2 * rows)
-    mlp_dup = ring.scatter_sum([dup], order_b, 2 * rows)
-    ddown_left = ring.scatter_sum([ddown[:, :half]], order_a, units)
-    ddown_right = ring.scatter_sum([ddown[:, half:]], order_b, units)
-    mlp_ddown = jnp.concatenate([ddown_left, ddown_right], axis=1)
-
     def own_columns(values):
         return lax.dynamic_slice_in_dim(values, ring.half * half, half, 1)
 
@@ -569,8 +823,7 @@
     dquery_two = dot_tn(normed_two, dquery).astype(LOW)
     dkey_two = dot_tn(patch_rows, dkey).astype(LOW)
     dvalue_two = dot_tn(patch_rows, dvalue).astype(LOW)
-    cross_a = ring.scatter_sum([dout_two, dquery_two], order_a, 2 * rows)
-    cross_b = ring.scatter_sum([dkey_two, dvalue_two], order_b, 2 * rows)
+    cross_sum = ring.scatter_sum([[dout_two, dquery_two], [dkey_two, dvalue_two]], 2 * rows)
 
     def to_owner(part, count):
         part = part.reshape(ring.groups, 2, count, width)
@@ -607,34 +860,37 @@
     self_dgain = jnp.sum(part_one * plain_one, axis=0)
     dgains = jnp.stack([self_dgain, cross_dgain, mlp_dgain], axis=1)
     dgains = jnp.pad(dgains, ((0, 0), (0, PAIR_LANES - 3))).astype(LOW)
-    self_a = ring.scatter_sum([dquery_one, dout_one, dgains], order_a, 2 * rows)
-    self_b = ring.scatter_sum([dkey_one, dvalue_one], order_b, 2 * rows)
+    self_sum = ring.scatter_sum(
+        [[dquery_one, dout_one, dgains], [dkey_one, dvalue_one]], 2 * rows
+    )
     dnormed_one = to_owner(part_one, own)
     last = norm_back(
         own_rows(plain_one[:both], own), own_rows(inverse_one[:both], own), gain_one, dnormed_one
     )
     input_grad = own_rows(dhidden_one, own) + last
 
-    def split(block, widths):
-        cuts = [sum(widths[:i]) for i in range(len(widths) + 1)]
-        return [block[:, cuts[i] : cuts[i + 1]] for i in range(len(widths))]
-
-    def finished(block, widths):
+    def finished(block, count):
         first, later = ring.unhalve(block)
-        pieces = zip(split(first, widths), split(later, widths))
-        return [jnp.concatenate(pair, axis=1) for pair in pieces]
-
-    mlp_dgate = unit_whole(*ring.unhalve(mlp_dgate), units)
-    mlp_dup = unit_whole(*ring.unhalve(mlp_dup), units)
-    cross_dout, cross_dquery = finished(cross_a, [half] * 2)
-    cross_dkey, cross_dvalue = finished(cross_b, [half] * 2)
-    self_first, self_later = ring.unhalve(self_a)
-    dgain_columns = self_first[:, 2 * half : 2 * half + 3] + self_later[:, 2 * half : 2 * half + 3]
-    self_dquery = jnp.concatenate([self_first[:, :half], self_later[:, :half]], axis=1)
-    self_dout = jnp.concatenate(
-        [self_first[:, half : 2 * half], self_later[:, half : 2 * half]], axis=1
-    )
-    self_dkey, self_dvalue = finished(self_b, [half] * 2)
+        return [
+            jnp.concatenate([part[:, i * half : (i + 1) * half] for part in (first, later)], axis=1)
+            for i in range(count)
+        ]
+
+    first, later = ring.unhalve(gate_up)
+    mlp_dgate = unit_whole(first[:, :hidden_half], later[:, :hidden_half], units)
+    mlp_dup = unit_whole(first[:, hidden_half:], later[:, hidden_half:], units)
+    cross_dout, cross_dquery, cross_dkey, cross_dvalue = finished(cross_sum, 4)
+    gain_at = 2 * half
+    dgain_block = self_sum[:, gain_at : gain_at + PAIR_LANES]
+    weights_sum = jnp.concatenate(
+        [self_sum[:, :gain_at], self_sum[:, gain_at + PAIR_LANES :], dgain_block], axis=1
+    )
+    first, later = ring.unhalve(weights_sum)
+    pick = lambda i: jnp.concatenate(
+        [part[:, i * half : (i + 1) * half] for part in (first, later)], axis=1
+    )
+    self_dquery, self_dout, self_dkey, self_dvalue = (pick(i) for i in range(4))
+    dgain_columns = first[:, 4 * half : 4 * half + 3] + later[:, 4 * half : 4 * half + 3]
 
     return (
         output[None],
@@ -658,9 +914,12 @@
 
 
 def solution(mesh):
-    rows = P(("dp", "head"), None)
-    vector = P(("dp", "head"))
-    grid = P("dp", "head", None)
+    charts, heads = mesh.devices.shape
+    inner = Mesh(mesh.devices.reshape(charts, heads // 2, 2), ("dp", "hx", "hc"))
+    every = ("dp", "hx", "hc")
+    rows = P(every, None)
+    vector = P(every)
+    grid = P("dp", ("hx", "hc"), None)
     in_specs = (grid, grid, P("dp"), P("dp"))
     in_specs += (vector, rows, rows, rows, rows) * 2
     in_specs += (vector, rows, rows, rows, grid)
@@ -668,5 +927,5 @@
     out_specs += (vector, rows, rows, rows, rows) * 2
     out_specs += (vector, rows, rows, rows)
     return jax.shard_map(
-        on_device, mesh=mesh, in_specs=in_specs, out_specs=out_specs, check_vma=False
-    )
+        on_device, mesh=inner, in_specs=in_specs, out_specs=out_specs, check_vma=False
+    )

time: 551 us -> 414 us (0.75)
  waiting for transfers between devices: 185 us -> 119 us
  starting transfers between devices: 92.7 us -> 40.4 us
  local copies, waits for them, and re-layouts: 60 us -> 33.6 us
  Pallas kernels: 74 us -> 96.4 us
  matrix products: 62.6 us -> 45.7 us
  between operations: 4.24 us -> 17.3 us
  other arithmetic: 63.5 us -> 57.8 us
    ppermute x92 -> x28, waiting for transfers between devices: 185 us -> 119 us  [send(): return lax.ppermute(values, axis, [(i, i ^ bit) for i in range(size)])]
    ppermute x92 -> x28, starting transfers between devices: 92.7 us -> 36.9 us  [send(): return lax.ppermute(values, axis, [(i, i ^ bit) for i in range(size)])]
    pallas_call x0 -> x3, Pallas kernels: none -> 17.2 us  [the longest x1 13.2 us: feed_forward(): pl.pallas_call(functools.partial(mlp_kernel, 256), out_shape=[big, big, j...]
    pallas_call x2, Pallas kernels: 20.9 us -> 34.7 us  [attention_backward(): pl.pallas_call(functools.partial(backward_kernel, causal, chunk), out_sha...]
    unnamed x234 -> x195, local copies, waits for them, and re-layouts: 31.5 us -> 18.5 us
    concatenate x8 -> x2, local copies, waits for them, and re-layouts: 10.8 us -> 0.05 us  [gather(): blocks = jnp.concatenate([blocks, self.send(blocks, axis, bit)], axis=0)]
    convert_element_type x24 -> x7, other arithmetic: 16.9 us -> 6.27 us  [the longest x4 4.33 us: scatter_sum(): keeps[side] = add(keeps[side][:half], got[:half]).astype(LOW)]
    pallas_call x8 -> x4, Pallas kernels: 19.4 us -> 9.68 us  [to_halves(): pl.pallas_call(functools.partial(halves_kernel, count, rows, cuts_of(widt...]
  transfers between devices with their start and end apart: 92 -> 46, of which waited for: 45 -> 18; matrix products, arithmetic and copies ran while one was open for 28% -> 28% of each run, Pallas kernels for 13% -> 20%
where the time goes in v2:
time: 414 us; the launch traced here: 410 us
  waiting for transfers between devices  119 us (29%)
  Pallas kernels  96.4 us (23%)
  other arithmetic  57.8 us (14%)
  matrix products  45.7 us (11%)
  starting transfers between devices  40.4 us (10%)
  local copies, waits for them, and re-layouts  33.6 us (8%)
  between operations  17.3 us (4%)
    ppermute x28, waiting for transfers between devices, send(): return lax.ppermute(values, axis, [(i, i ^ bit) for i in range(size)])  119 us
    ppermute x28, starting transfers between devices, send(): return lax.ppermute(values, axis, [(i, i ^ bit) for i in range(size)])  36.9 us
    pallas_call x2, Pallas kernels, attention_backward(): pl.pallas_call(functools.partial(backward_kernel, causal, chunk), out_sha...  34.7 us
    pallas_call x2, Pallas kernels, attention_forward(): pl.pallas_call(functools.partial(forward_kernel, causal, chunk), out_shap...  23.6 us
    dot_general x8, matrix products, dot_nt(): return lax.dot_general(left, right, NT, preferred_element_type=F32)  19.6 us
    unnamed x195, local copies, waits for them, and re-layouts  18.5 us
    dot_general x8, matrix products, dot_tn(): return lax.dot_general(left, right, TN, preferred_element_type=F32)  15.9 us
    pallas_call x1, Pallas kernels, feed_forward(): pl.pallas_call(functools.partial(mlp_kernel, 256), out_shape=[big, big, j...  13.2 us
  transfers between devices with their start and end apart: 46, of which 18 were waited for; matrix products, arithmetic and copies ran while one was open for 28% of the time, Pallas kernels for 20%

profile of v2, /device:TPU:0, one launch (start us, length us, event | category | flops | bytes accessed | tf_op | source)
XLA Modules:
  0.0 410.5 jit_solution(13717449531776411909)
XLA Ops:
  25.7 6.0 %collective-permute-done.3 = bf16[1,48,1280]{2,1,0:T(8,128)(2,1)S(1)} collective-permute-done((bf16[1,48,1280]{2,1,0:T(8,128)(2,1)}, bf16[1,48,1280]{2,1,0:T(8,128)(2,1)S(1)}, u32[]{:S(2)}, u32[]{:S(2)}) %collective-permute-start.3) | collective-permute-done | bytes 122912 | tf_op jit(solution)/shard_map/ppermute | solution.py:521
  35.4 7.3 %collective-permute-done = bf16[1,256,768]{2,1,0:T(8,128)(2,1)S(1)} collective-permute-done((bf16[1,256,768]{2,1,0:T(8,128)(2,1)}, bf16[1,256,768]{2,1,0:T(8,128)(2,1)S(1)}, u32[]{:S(2)}, u32[]{:S(2)}) %collective-permute-start) | collective-permute-done | bytes 393248 | tf_op jit(solution)/shard_map/ppermute | solution.py:521
  45.8 16.2 %collective-permute-done.4 = bf16[2,48,1280]{2,1,0:T(8,128)(2,1)S(1)} collective-permute-done((bf16[2,48,1280]{2,1,0:T(8,128)(2,1)S(1)}, bf16[2,48,1280]{2,1,0:T(8,128)(2,1)S(1)}, u32[]{:S(2)}, u32[]{:S(2)}) %collective-permute-start.4) | collective-permute-done | bytes 245792 | tf_op jit(solution)/shard_map/ppermute | solution.py:521
  63.6 5.3 %collective-permute-done.11 = bf16[2,48,1920]{2,1,0:T(8,128)(2,1)S(1)} collective-permute-done((bf16[2,48,1920]{2,1,0:T(8,128)(2,1)S(1)}, bf16[2,48,1920]{2,1,0:T(8,128)(2,1)S(1)}, u32[]{:S(2)}, u32[]{:S(2)}) %collective-permute-start.11) | collective-permute-done | bytes 368672 | tf_op jit(solution)/shard_map/ppermute | solution.py:521
  74.1 9.2 %collective-permute-done.7 = bf16[4,48,768]{2,1,0:T(8,128)(2,1)S(1)} collective-permute-done((bf16[4,48,768]{2,1,0:T(8,128)(2,1)S(1)}, bf16[4,48,768]{2,1,0:T(8,128)(2,1)S(1)}, u32[]{:S(2)}, u32[]{:S(2)}) %collective-permute-start.7) | collective-permute-done | bytes 294944 | tf_op jit(solution)/shard_map/ppermute | solution.py:521
  85.7 3.3 collective-permute-done.17
  93.2 11.1 %collective-permute-done.6.later = bf16[8,48,512]{2,1,0:T(8,128)(2,1)S(1)} collective-permute-done((bf16[8,48,512]{2,1,0:T(8,128)(2,1)S(1)}, bf16[8,48,512]{2,1,0:T(8,128)(2,1)S(1)}, u32[]{:S(2)}, u32[]{:S(2)}) %collective-permute-start.6) | collective-permute-done | bytes 393248 | tf_op jit(solution)/shard_map/ppermute | solution.py:521
  115.0 7.3 %collective-permute-done.8.later = bf16[8,48,768]{2,1,0:T(8,128)(2,1)} collective-permute-done((bf16[8,48,768]{2,1,0:T(8,128)(2,1)}, bf16[8,48,768]{2,1,0:T(8,128)(2,1)}, u32[]{:S(2)}, u32[]{:S(2)}) %collective-permute-start.8) | collective-permute-done | bytes 589856 | tf_op jit(solution)/shard_map/ppermute | solution.py:521
  128.7 5.8 %shard_map.354 = (bf16[512,384]{1,0:T(8,128)(2,1)S(1)}, f32[3,2,512]{2,1,0:T(2,128)S(1)}) custom-call(s32[6]{0:T(128)S(1)} %pad_add_fusion.info, bf16[512,384]{1,0:T(8,128)(2,1)S(1)} %convolution_convert_fusion.15.q_ref, bf16[1024,384]{1,0:T(8,128)(2,1)S(1)} %convolution_convert_fusion.3.k_ref, bf16[1024,384]{1,0:T(8,128)(2,1)S(1)} %convolution_convert_fusion.2.v_ref), custom_call_target="tpu_custom_call" | custom-call | flops 3221225472 | bytes 2359296 | tf_op jit(solution)/shard_map/pallas_call | solution.py:162
  143.0 3.5 shard_map.355
  157.9 17.9 %shard_map.357 = (bf16[512,384]{1,0:T(8,128)(2,1)S(1)}, f32[3,2,512]{2,1,0:T(2,128)S(1)}) custom-call(s32[10]{0:T(128)S(1)} %pad_add_fusion.1.info, bf16[512,384]{1,0:T(8,128)(2,1)S(1)} %convolution_convert_fusion.14.q_ref, bf16[2048,384]{1,0:T(8,128)(2,1)S(1)} %convolution_convert_fusion.1.k_ref, bf16[2048,384]{1,0:T(8,128)(2,1)S(1)} %convolution_convert_fusion.v_ref), custom_call_target="tpu_custom_call" | custom-call | flops 6442450944 | bytes 3932160 | tf_op jit(solution)/shard_map/pallas_call | solution.py:162
  183.3 13.2 %shard_map.358 = (f32[512,768]{1,0:T(8,128)S(1)}, f32[512,768]{1,0:T(8,128)S(1)}, bf16[16,16,9216]{2,1,0:T(8,128)(2,1)}) custom-call(bf16[512,768]{1,0:T(8,128)(2,1)S(1)} %copy-done.1, bf16[512,768]{1,0:T(8,128)(2,1)S(1)} %copy-done, bf16[16,16,9216]{2,1,0:T(8,128)(2,1)} %bitcast.136), custom_call_target="tpu_custom_call" | custom-call | flops 7247757312 | bytes 14155776 | tf_op jit(solution)/shard_map/pallas_call | solution.py:461
  214.7 26.0 %shard_map.359 = (bf16[512,384]{1,0:T(8,128)(2,1)S(1)}, bf16[2048,384]{1,0:T(8,128)(2,1)S(1)}, bf16[2048,384]{1,0:T(8,128)(2,1)S(1)}) custom-call(s32[10]{0:T(128)S(1)} %pad_add_fusion.1.info, bf16[512,384]{1,0:T(8,128)(2,1)S(1)} %copy-done.5, bf16[2048,384]{1,0:T(8,128)(2,1)S(1)} %copy-done.15, bf16[2048,384]{1,0:T(8,128)(2,1)S(1)} %copy-done.13, ...), custom_call_target="tpu_custom_call" | custom-call | flops 16106127360 | bytes 7864320 | tf_op jit(solution)/shard_map/pallas_call | solution.py:193
  247.7 4.5 %fusion.58 = f32[2048,768]{1,0:T(8,128)} fusion(bf16[2048,384]{1,0:T(8,128)(2,1)S(1)} %get-tuple-element.77, bf16[768,384]{1,0:T(8,128)(2,1)S(1)} %copy-done.55), kind=kOutput, calls=%fused_computation.233 | convolution fusion | flops 1207959552 | bytes 8454144 | tf_op jit(solution)/shard_map/dot_general | solution.py:25
  260.4 5.1 %convolution_add_fusion = f32[2048,768]{1,0:T(8,128)S(1)} fusion(f32[2048,768]{1,0:T(8,128)} %fusion.58, bf16[2048,384]{1,0:T(8,128)(2,1)S(1)} %get-tuple-element.76, bf16[768,384]{1,0:T(8,128)(2,1)} %get-tuple-element.63), kind=kOutput, calls=%fused_computation | convolution fusion | flops 1209532416 | bytes 14745600 | tf_op jit(solution)/shard_map/dot_general | solution.py:25
  267.2 9.2 %collective-permute-done.38 = bf16[8,48,768]{2,1,0:T(8,128)(2,1)} collective-permute-done((bf16[8,48,768]{2,1,0:T(8,128)(2,1)}, bf16[8,48,768]{2,1,0:T(8,128)(2,1)}, u32[]{:S(2)}, u32[]{:S(2)}) %collective-permute-start.38) | collective-permute-done | bytes 589856 | tf_op jit(solution)/shard_map/ppermute | solution.py:521
  286.8 8.7 %shard_map.360 = (bf16[512,384]{1,0:T(8,128)(2,1)S(1)}, bf16[1024,384]{1,0:T(8,128)(2,1)S(1)}, bf16[1024,384]{1,0:T(8,128)(2,1)S(1)}) custom-call(s32[6]{0:T(128)S(1)} %pad_add_fusion.info, bf16[512,384]{1,0:T(8,128)(2,1)S(1)} %copy-done.7, bf16[1024,384]{1,0:T(8,128)(2,1)S(1)} %copy-done.11, bf16[1024,384]{1,0:T(8,128)(2,1)S(1)} %copy-done.9, ...), custom_call_target="tpu_custom_call" | custom-call | flops 8053063680 | bytes 4718592 | tf_op jit(solution)/shard_map/pallas_call | solution.py:193
  306.2 3.6 convolution_add_fusion.1
  322.6 5.3 %collective-permute-start.29 = (bf16[8,48,896]{2,1,0:T(8,128)(2,1)}, bf16[8,48,896]{2,1,0:T(8,128)(2,1)S(1)}, u32[]{:S(2)}, u32[]{:S(2)}) collective-permute-start(bf16[8,48,896]{2,1,0:T(8,128)(2,1)} %get-tuple-element.79), channel_id=1, source_target_pairs={{0,2},{2,0},{1,3},{3,1},{4,6},{6,4},{5,7},{7,5},{8,10},{10,8},{9,1... | collective-permute-start | bytes 2064392 | tf_op jit(solution)/shard_map/ppermute | solution.py:521
  328.0 11.1 %collective-permute-done.40 = bf16[2,48,1536]{2,1,0:T(8,128)(2,1)} collective-permute-done((bf16[2,48,1536]{2,1,0:T(8,128)(2,1)}, bf16[2,48,1536]{2,1,0:T(8,128)(2,1)}, u32[]{:S(2)}, u32[]{:S(2)}) %collective-permute-start.40) | collective-permute-done | bytes 294944 | tf_op jit(solution)/shard_map/ppermute | solution.py:521
  342.4 4.8 %collective-permute-done.41 = bf16[1,48,1536]{2,1,0:T(8,128)(2,1)S(1)} collective-permute-done((bf16[1,48,1536]{2,1,0:T(8,128)(2,1)S(1)}, bf16[1,48,1536]{2,1,0:T(8,128)(2,1)S(1)}, u32[]{:S(2)}, u32[]{:S(2)}) %collective-permute-start.41) | collective-permute-done | bytes 147488 | tf_op jit(solution)/shard_map/ppermute | solution.py:521
  361.5 3.8 collective-permute-done.30
  367.0 19.8 %collective-permute-done.26 = bf16[1,256,768]{2,1,0:T(8,128)(2,1)S(1)} collective-permute-done((bf16[1,256,768]{2,1,0:T(8,128)(2,1)S(1)}, bf16[1,256,768]{2,1,0:T(8,128)(2,1)S(1)}, u32[]{:S(2)}, u32[]{:S(2)}) %collective-permute-start.26) | collective-permute-done | bytes 393248 | tf_op jit(solution)/shard_map/ppermute | solution.py:521
  389.2 3.2 collective-permute-done.34
  (434 shorter events, 182.2 us)
Async XLA Ops:
  7.2 173.8 %all-gather.2.cloned.1.call-start = ((), (), s32[]{:S(2)}) async-start(), calls=%async_computation.1 | async-start | bytes 5013504 | tf_op jit(solution)/shard_map/all_gather | solution.py:689
  11.2 59.2 %collective-permute-start.15 = (bf16[1,512,768]{2,1,0:T(8,128)(2,1)}, bf16[1,512,768]{2,1,0:T(8,128)(2,1)}, u32[]{:S(2)}, u32[]{:S(2)}) collective-permute-start(bf16[1,512,768]{2,1,0:T(8,128)(2,1)} %param.24), channel_id=1, source_target_pairs={{0,2},{2,0},{1,3},{3,1},{4,6},{6,4},{5,7},{7,5},{8,10},{10,8},{9,1... | collective-permute-start | bytes 2359304 | tf_op jit(solution)/shard_map/ppermute | solution.py:521
  13.7 28.9 %collective-permute-start = (bf16[1,256,768]{2,1,0:T(8,128)(2,1)}, bf16[1,256,768]{2,1,0:T(8,128)(2,1)S(1)}, u32[]{:S(2)}, u32[]{:S(2)}) collective-permute-start(bf16[1,256,768]{2,1,0:T(8,128)(2,1)} %param.23), channel_id=1, source_target_pairs={{0,2},{2,0},{1,3},{3,1},{4,6},{6,4},{5,7},{7,5},{8,10},{10,8},{9,1... | collective-permute-start | bytes 1179656 | tf_op jit(solution)/shard_map/ppermute | solution.py:521
  13.8 122.2 %collective-permute-start.21 = (bf16[256,768]{1,0:T(8,128)(2,1)}, bf16[256,768]{1,0:T(8,128)(2,1)}, u32[]{:S(2)}, u32[]{:S(2)}) collective-permute-start(bf16[256,768]{1,0:T(8,128)(2,1)} %bitcast.130), channel_id=1, source_target_pairs={{0,1},{1,0},{2,3},{3,2},{4,5},{5,4},{6,7},{7,6},{8,9},{9,8},{10,11... | collective-permute-start | bytes 1179656 | tf_op jit(solution)/shard_map/ppermute | solution.py:524
  24.7 372.7 %reduce-scatter.2.cloned.1.call-start = ((), (), s32[]{:S(2)}) async-start(), calls=%async_computation.2 | async-start | bytes 5013504 | tf_op jit(solution)/shard_map/reduce_scatter | solution.py:760
  32.6 29.3 %collective-permute-start.4 = (bf16[2,48,1280]{2,1,0:T(8,128)(2,1)S(1)}, bf16[2,48,1280]{2,1,0:T(8,128)(2,1)S(1)}, u32[]{:S(2)}, u32[]{:S(2)}) collective-permute-start(bf16[2,48,1280]{2,1,0:T(8,128)(2,1)S(1)} %pad_maximum_fusion.25), channel_id=1, source_target_pairs={{0,16},{4,20},{8,24},{12,28},{16,0},{20,4},{24,8},{28,12},{1,17},{... | collective-permute-start | bytes 737288 | tf_op jit(solution)/shard_map/ppermute | solution.py:521
  42.7 47.5 %collective-permute-start.1 = (bf16[2,256,768]{2,1,0:T(8,128)(2,1)S(1)}, bf16[2,256,768]{2,1,0:T(8,128)(2,1)S(1)}, u32[]{:S(2)}, u32[]{:S(2)}) collective-permute-start(bf16[2,256,768]{2,1,0:T(8,128)(2,1)S(1)} %constant_dynamic-update-slice_fusion), channel_id=1, source_target_pairs={{0,1},{1,0},{2,3},{3,2},{4,5},{5,4},{6,7},{7,6},{8,9},{9,8},{10,11... | collective-permute-start | bytes 2359304 | tf_op jit(solution)/shard_map/ppermute | solution.py:524
  42.8 26.1 %collective-permute-start.11 = (bf16[2,48,1920]{2,1,0:T(8,128)(2,1)S(1)}, bf16[2,48,1920]{2,1,0:T(8,128)(2,1)S(1)}, u32[]{:S(2)}, u32[]{:S(2)}) collective-permute-start(bf16[2,48,1920]{2,1,0:T(8,128)(2,1)S(1)} %pad_maximum_fusion.19), channel_id=1, source_target_pairs={{0,16},{4,20},{8,24},{12,28},{16,0},{20,4},{24,8},{28,12},{1,17},{... | collective-permute-start | bytes 1105928 | tf_op jit(solution)/shard_map/ppermute | solution.py:521
  74.0 73.0 %collective-permute-start.16 = (bf16[2,512,768]{2,1,0:T(8,128)(2,1)}, bf16[2,512,768]{2,1,0:T(8,128)(2,1)}, u32[]{:S(2)}, u32[]{:S(2)}) collective-permute-start(bf16[2,512,768]{2,1,0:T(8,128)(2,1)} %constant_dynamic-update-slice_fusion.8), channel_id=1, source_target_pairs={{0,1},{1,0},{2,3},{3,2},{4,5},{5,4},{6,7},{7,6},{8,9},{9,8},{10,11... | collective-permute-start | bytes 4718600 | tf_op jit(solution)/shard_map/ppermute | solution.py:524
  83.3 29.7 %collective-permute-start.12 = (bf16[4,48,1152]{2,1,0:T(8,128)(2,1)}, bf16[4,48,1152]{2,1,0:T(8,128)(2,1)}, u32[]{:S(2)}, u32[]{:S(2)}) collective-permute-start(bf16[4,48,1152]{2,1,0:T(8,128)(2,1)} %slice.438), channel_id=1, source_target_pairs={{0,4},{4,0},{8,12},{12,8},{16,20},{20,16},{24,28},{28,24},{1,5},{5... | collective-permute-start | bytes 1327112 | tf_op jit(solution)/shard_map/ppermute | solution.py:521
  90.2 32.2 %collective-permute-start.8 = (bf16[8,48,768]{2,1,0:T(8,128)(2,1)}, bf16[8,48,768]{2,1,0:T(8,128)(2,1)}, u32[]{:S(2)}, u32[]{:S(2)}) collective-permute-start(bf16[8,48,768]{2,1,0:T(8,128)(2,1)} %pad_maximum_fusion.10.first), channel_id=1, source_target_pairs={{0,4},{4,0},{8,12},{12,8},{16,20},{20,16},{24,28},{28,24},{1,5},{5... | collective-permute-start | bytes 1769480 | tf_op jit(solution)/shard_map/ppermute | solution.py:521
  105.0 32.1 %collective-permute-start.18 = (bf16[8,48,768]{2,1,0:T(8,128)(2,1)}, bf16[8,48,768]{2,1,0:T(8,128)(2,1)}, u32[]{:S(2)}, u32[]{:S(2)}) collective-permute-start(bf16[8,48,768]{2,1,0:T(8,128)(2,1)} %pad_maximum_fusion.11.first), channel_id=1, source_target_pairs={{0,4},{4,0},{8,12},{12,8},{16,20},{20,16},{24,28},{28,24},{1,5},{5... | collective-permute-start | bytes 1769480 | tf_op jit(solution)/shard_map/ppermute | solution.py:521
  114.4 27.7 %collective-permute-start.13 = (bf16[8,48,1152]{2,1,0:T(8,128)(2,1)S(1)}, bf16[8,48,1152]{2,1,0:T(8,128)(2,1)S(1)}, u32[]{:S(2)}, u32[]{:S(2)}) collective-permute-start(bf16[8,48,1152]{2,1,0:T(8,128)(2,1)S(1)} %pad_maximum_fusion.6.first), channel_id=1, source_target_pairs={{0,2},{2,0},{1,3},{3,1},{4,6},{6,4},{5,7},{7,5},{8,10},{10,8},{9,1... | collective-permute-start | bytes 2654216 | tf_op jit(solution)/shard_map/ppermute | solution.py:521
  146.9 30.4 %collective-permute-start.20 = (bf16[768,384]{1,0:T(8,128)(2,1)}, bf16[768,384]{1,0:T(8,128)(2,1)S(1)}, u32[]{:S(2)}, u32[]{:S(2)}) collective-permute-start(bf16[768,384]{1,0:T(8,128)(2,1)} %get-tuple-element.66), channel_id=1, source_target_pairs={{0,1},{1,0},{2,3},{3,2},{4,5},{5,4},{6,7},{7,6},{8,9},{9,8},{10,11... | collective-permute-start | bytes 1769480 | tf_op jit(solution)/shard_map/ppermute | solution.py:524
  260.2 21.9 %collective-permute-start.24 = (bf16[512,768]{1,0:T(8,128)(2,1)}, bf16[512,768]{1,0:T(8,128)(2,1)S(1)}, u32[]{:S(2)}, u32[]{:S(2)}) collective-permute-start(bf16[512,768]{1,0:T(8,128)(2,1)} %get-tuple-element.181), channel_id=1, source_target_pairs={{0,1},{1,0},{2,3},{3,2},{4,5},{5,4},{6,7},{7,6},{8,9},{9,8},{10,11... | collective-permute-start | bytes 2359304 | tf_op jit(solution)/shard_map/ppermute | solution.py:524
  267.0 89.7 %collective-permute-start.27 = (bf16[2,512,768]{2,1,0:T(8,128)(2,1)}, bf16[2,512,768]{2,1,0:T(8,128)(2,1)}, u32[]{:S(2)}, u32[]{:S(2)}) collective-permute-start(bf16[2,512,768]{2,1,0:T(8,128)(2,1)} %fusion), channel_id=1, source_target_pairs={{0,1},{1,0},{2,3},{3,2},{4,5},{5,4},{6,7},{7,6},{8,9},{9,8},{10,11... | collective-permute-start | bytes 4718600 | tf_op jit(solution)/shard_map/ppermute | solution.py:524
  278.5 35.2 %collective-permute-start.39 = (bf16[4,48,768]{2,1,0:T(8,128)(2,1)}, bf16[4,48,768]{2,1,0:T(8,128)(2,1)}, u32[]{:S(2)}, u32[]{:S(2)}) collective-permute-start(bf16[4,48,768]{2,1,0:T(8,128)(2,1)} %get-tuple-element.114), channel_id=1, source_target_pairs={{0,2},{2,0},{1,3},{3,1},{4,6},{6,4},{5,7},{7,5},{8,10},{10,8},{9,1... | collective-permute-start | bytes 884744 | tf_op jit(solution)/shard_map/ppermute | solution.py:521
  280.6 34.2 %collective-permute-start.37 = (bf16[4,48,768]{2,1,0:T(8,128)(2,1)}, bf16[4,48,768]{2,1,0:T(8,128)(2,1)}, u32[]{:S(2)}, u32[]{:S(2)}) collective-permute-start(bf16[4,48,768]{2,1,0:T(8,128)(2,1)} %get-tuple-element.116), channel_id=1, source_target_pairs={{0,4},{4,0},{8,12},{12,8},{16,20},{20,16},{24,28},{28,24},{1,5},{5... | collective-permute-start | bytes 884744 | tf_op jit(solution)/shard_map/ppermute | solution.py:521
  305.7 42.7 %collective-permute-start.31 = (bf16[8,48,768]{2,1,0:T(8,128)(2,1)}, bf16[8,48,768]{2,1,0:T(8,128)(2,1)}, u32[]{:S(2)}, u32[]{:S(2)}) collective-permute-start(bf16[8,48,768]{2,1,0:T(8,128)(2,1)} %get-tuple-element.81), channel_id=1, source_target_pairs={{0,4},{4,0},{8,12},{12,8},{16,20},{20,16},{24,28},{28,24},{1,5},{5... | collective-permute-start | bytes 1769480 | tf_op jit(solution)/shard_map/ppermute | solution.py:521
  316.6 22.5 %collective-permute-start.40 = (bf16[2,48,1536]{2,1,0:T(8,128)(2,1)}, bf16[2,48,1536]{2,1,0:T(8,128)(2,1)}, u32[]{:S(2)}, u32[]{:S(2)}) collective-permute-start(bf16[2,48,1536]{2,1,0:T(8,128)(2,1)} %pad_maximum_fusion.24), channel_id=1, source_target_pairs={{0,16},{4,20},{8,24},{12,28},{16,0},{20,4},{24,8},{28,12},{1,17},{... | collective-permute-start | bytes 884744 | tf_op jit(solution)/shard_map/ppermute | solution.py:521
  322.6 32.3 %collective-permute-start.29 = (bf16[8,48,896]{2,1,0:T(8,128)(2,1)}, bf16[8,48,896]{2,1,0:T(8,128)(2,1)S(1)}, u32[]{:S(2)}, u32[]{:S(2)}) collective-permute-start(bf16[8,48,896]{2,1,0:T(8,128)(2,1)} %get-tuple-element.79), channel_id=1, source_target_pairs={{0,2},{2,0},{1,3},{3,1},{4,6},{6,4},{5,7},{7,5},{8,10},{10,8},{9,1... | collective-permute-start | bytes 2064392 | tf_op jit(solution)/shard_map/ppermute | solution.py:521
  358.9 33.7 %collective-permute-start.28 = (bf16[1,512,768]{2,1,0:T(8,128)(2,1)S(1)}, bf16[1,512,768]{2,1,0:T(8,128)(2,1)S(1)}, u32[]{:S(2)}, u32[]{:S(2)}) collective-permute-start(bf16[1,512,768]{2,1,0:T(8,128)(2,1)S(1)} %slice.681), channel_id=1, source_target_pairs={{0,2},{2,0},{1,3},{3,1},{4,6},{6,4},{5,7},{7,5},{8,10},{10,8},{9,1... | collective-permute-start | bytes 2359304 | tf_op jit(solution)/shard_map/ppermute | solution.py:521
  359.3 27.4 %collective-permute-start.26 = (bf16[1,256,768]{2,1,0:T(8,128)(2,1)S(1)}, bf16[1,256,768]{2,1,0:T(8,128)(2,1)S(1)}, u32[]{:S(2)}, u32[]{:S(2)}) collective-permute-start(bf16[1,256,768]{2,1,0:T(8,128)(2,1)S(1)} %slice.682), channel_id=1, source_target_pairs={{0,2},{2,0},{1,3},{3,1},{4,6},{6,4},{5,7},{7,5},{8,10},{10,8},{9,1... | collective-permute-start | bytes 1179656 | tf_op jit(solution)/shard_map/ppermute | solution.py:521
  365.5 21.5 %collective-permute-start.33 = (bf16[2,48,1664]{2,1,0:T(8,128)(2,1)S(1)}, bf16[2,48,1664]{2,1,0:T(8,128)(2,1)S(1)}, u32[]{:S(2)}, u32[]{:S(2)}) collective-permute-start(bf16[2,48,1664]{2,1,0:T(8,128)(2,1)S(1)} %pad_maximum_fusion.21), channel_id=1, source_target_pairs={{0,16},{4,20},{8,24},{12,28},{16,0},{20,4},{24,8},{28,12},{1,17},{... | collective-permute-start | bytes 958472 | tf_op jit(solution)/shard_map/ppermute | solution.py:521
  (116 other events, 870.0 us)
Sparse Core Ops, SparseCore 0:
  24.8 117.9 all-gather.1
  204.0 150.7 reduce-scatter.1
